TPU v7x, 32 devices: a whole 2x2x4 slice. The times are simulated.
32 devices in a mesh: lat: 4 (over y, x), lon: 8 (over z, core).
Axes of the slice: x: 2, y: 2, z: 4, core: 2. Of those that a mesh axis runs over, the one named last changes fastest.
Arguments:
- predicted_quantities: bfloat16 [3, 8, 256, 4096], P(None, None, 'lat', 'lon'), may hold values from -60 to 60
- monitor_coefficients: float32 [8], replicated, may hold values from 0.2 to 2
- departing_pieces: int32 [4, 8, 8, 32], P('lat', 'lon'), may hold values from 0 to 255
- departing_occupancy: int32 [4, 8, 8], P('lat', 'lon'), may hold values from 1 to 32, as said below
- arriving_pieces: int32 [4, 8, 8, 32], P('lat', 'lon'), may hold values from 0 to 255
- interpolant_coefficients: bfloat16 [4, 8, 8, 32, 128, 128], P('lat', 'lon'), may hold values from -0.5 to 0.5
Outputs:
- potential: float32 [256, 4096], P('lat', 'lon')
- scaled_residual: float32 [256, 4096], P('lat', 'lon')
Inputs may be any that keep to these rules, and one draw needn't show every extreme that they name: `departing_occupancy`: in each lat row a quarter of the lon indices, drawn from the seed, receive 32 tiles from every device of the row; every other count is at most 16.
All inputs are finite; a program needn't handle non-finite values.
Results may differ from a plain program's by a relative error of at most 0.00087.
Values may be sent and summed in bfloat16 or wider, within the bound.
No kernel may reach another device: no remote copies, remote signals or barrier semaphores. Data moves between devices by JAX's collectives and lax.ppermute only.
A program may use at most 64 MiB of HBM per device.

v0:
```python
import functools

import jax
import jax.numpy as jnp
from jax import lax
from jax.experimental import pallas as pl
from jax.experimental.pallas import tpu as pltpu
from jax.sharding import PartitionSpec as P


FIELDS = 8
TILE = 128
CAP = 32
SWEEPS = 3


VMEM = pltpu.MemorySpace.VMEM
SMEM = pltpu.MemorySpace.SMEM


def to_tiles(pq_ref, out_ref):
    fields, rows, cols = pq_ref.shape
    blocks = cols // TILE
    for b in range(rows // 16):
        for c in range(blocks):
            part = pq_ref[:, b * 16 : b * 16 + 16, c * TILE : (c + 1) * TILE]
            part = jnp.transpose(part.astype(jnp.float32), (1, 0, 2))
            for i in range(16):
                start = ((b * 16 + i) * blocks + c) * fields
                out_ref[start : start + fields, :] = part[i]


def pack_tiles(lon, rows_ref, moved_ref, send_refs):
    for r, send_ref in enumerate(send_refs):
        dest = lon ^ r
        for k in range(0, CAP, 2):
            pair = []
            for i in (k, k + 1):
                start = pl.multiple_of(rows_ref[dest, i], FIELDS)
                pair.append(moved_ref[pl.ds(start, FIELDS), :])
            send_ref[k * FIELDS : (k + 2) * FIELDS, :] = jnp.concatenate(pair, axis=0).astype(
                jnp.bfloat16
            )


def zero_tile(moved_ref):
    moved_ref[moved_ref.shape[0] - FIELDS :, :] = jnp.zeros((FIELDS, TILE), jnp.float32)


def first_kernel(n_lon, *refs):
    ids_hbm, occ_hbm, targets_hbm, coef_hbm, pq_hbm = refs[:5]
    still_ref, rows_ref, targets_ref, coef_ref = refs[5:9]
    send_refs, (ids_ref, occ_ref, place_ref, pq_ref, sems) = refs[9:-5], refs[-5:]
    fields = pltpu.make_async_copy(pq_hbm.at[0], pq_ref, sems.at[0])
    lists = [
        pltpu.make_async_copy(ids_hbm, ids_ref, sems.at[1]),
        pltpu.make_async_copy(occ_hbm, occ_ref, sems.at[2]),
    ]
    later = [
        pltpu.make_async_copy(targets_hbm, targets_ref, sems.at[3]),
        pltpu.make_async_copy(coef_hbm, coef_ref, sems.at[4]),
    ]
    for copy in (*lists, fields, *later):
        copy.start()
    zero_tile(still_ref)
    for copy in lists:
        copy.wait()
    dest_id = lax.broadcasted_iota(jnp.int32, (n_lon, CAP), 0)
    slot_id = lax.broadcasted_iota(jnp.int32, (n_lon, CAP), 1)
    count = jnp.zeros((n_lon, CAP), jnp.int32)
    for d in range(n_lon):
        count = jnp.where(dest_id == d, occ_ref[d], count)
    zero_row = still_ref.shape[0] - FIELDS
    rows_ref[...] = jnp.where(slot_id < count, ids_ref[...] * FIELDS, zero_row)
    places = pltpu.make_async_copy(rows_ref, place_ref, sems.at[1])
    places.start()
    fields.wait()
    to_tiles(pq_ref, still_ref)
    places.wait()
    pack_tiles(lax.axis_index("lon"), place_ref, still_ref, send_refs)
    for copy in later:
        copy.wait()


def sum_fields(tiles):
    sub = lax.broadcasted_iota(jnp.int32, (8, TILE), 0)
    high = (sub & 4) == 0
    pairs = []
    for i in range(4):
        one, two = tiles[i], tiles[i + 4]
        kept, moving = jnp.where(high, one, two), jnp.where(high, two, one)
        pairs.append(kept + pltpu.roll(moving, 4, 0))
    for step in (2, 1):
        near = (sub & step) == 0
        pairs = [
            jnp.where(
                near,
                pairs[i] + pltpu.roll(pairs[i], 8 - step, 0),
                pairs[i + step] + pltpu.roll(pairs[i + step], step, 0),
            )
            for i in range(step)
        ]
    return pairs[0]


def column_to_lanes(column, offset):
    rows = column.shape[0]
    row_id = lax.broadcasted_iota(jnp.int32, (rows, TILE), 0)
    lane_id = lax.broadcasted_iota(jnp.int32, (rows, TILE), 1)
    wide = jnp.broadcast_to(column, (rows, TILE))
    return jnp.sum(jnp.where(lane_id == row_id + offset, wide, 0.0), axis=0, keepdims=True)


def lanes_to_column(lanes, rows, offset):
    row_id = lax.broadcasted_iota(jnp.int32, (rows, TILE), 0)
    lane_id = lax.broadcasted_iota(jnp.int32, (rows, TILE), 1)
    wide = jnp.broadcast_to(lanes, (rows, TILE))
    return jnp.sum(jnp.where(lane_id == row_id + offset, wide, 0.0), axis=1, keepdims=True)


def lane_value(lanes, index):
    lane_id = lax.broadcasted_iota(jnp.int32, lanes.shape, 1)
    return jnp.sum(jnp.where(lane_id == index, lanes, 0.0), axis=1, keepdims=True)


def mesh_place():
    lat, lon = lax.axis_index("lat"), lax.axis_index("lon")
    return lat, lon


def add_source(source, local, targets_ref, x_ref, w_ref, acc_ref):
    for k in range(0, CAP, 2):
        pair = jnp.concatenate([w_ref[local, k], w_ref[local, k + 1]], axis=1)
        out = jnp.dot(
            x_ref[k * FIELDS : (k + 2) * FIELDS, :], pair, preferred_element_type=jnp.float32
        )
        for i in (0, 1):
            start = pl.multiple_of(targets_ref[source, k + i] * FIELDS, FIELDS)
            acc_ref[pl.ds(start, FIELDS), :] += out[
                i * FIELDS : (i + 1) * FIELDS, i * TILE : (i + 1) * TILE
            ]


def groups(n_lon):
    half = n_lon // 2
    late = list(range(2, half)) + list(range(half, half + half // 2))
    return [r for r in [0, 1] + list(range(n_lon - 1, half - 1, -1)) if r not in late], late


def add_sources(n_lon, partners, targets_ref, x_refs, near_ref, far_ref, acc_ref):
    half = n_lon // 2
    lon = lax.axis_index("lon")
    for r, x_ref in zip(partners, x_refs):
        w_ref = near_ref if r < half else far_ref
        add_source(lon ^ r, (lon ^ r) & (half - 1), targets_ref, x_ref, w_ref, acc_ref)


def early_kernel(n_lon, start_sweep, *refs):
    half = n_lon // 2
    partners = groups(n_lon)[0]
    count = len(partners)
    targets_ref, moved_ref, x_refs, refs = refs[0], refs[1], refs[2 : 2 + count], refs[2 + count :]
    if start_sweep:
        pq_hbm, w_hbm, acc_ref, near_ref, far_ref, lon_ref, lat_ref, pq_ref, sems = refs
        mine = lax.axis_index("lon") & half
        far = pltpu.make_async_copy(w_hbm.at[pl.ds(half - mine, half)], far_ref, sems.at[0])
        near = pltpu.make_async_copy(w_hbm.at[pl.ds(mine, half)], near_ref, sems.at[1])
        parts = pltpu.make_async_copy(pq_hbm.at[pl.ds(1, 2)], pq_ref, sems.at[2])
        for copy in (parts, far, near):
            copy.start()
    else:
        near_ref, far_ref, acc_ref = refs
    acc_ref[...] = moved_ref[0 : acc_ref.shape[0], :]
    if start_sweep:
        parts.wait()
        to_tiles(pq_ref.at[0], lon_ref)
        to_tiles(pq_ref.at[1], lat_ref)
        far.wait()
        near.wait()
    add_sources(n_lon, partners, targets_ref, x_refs, near_ref, far_ref, acc_ref)


def late_kernel(n_lat, n_lon, start_sweep, *refs):
    partners = groups(n_lon)[1]
    count = len(partners)
    targets_ref, coef_ref, moved_ref, near_ref, far_ref = refs[:5]
    x_refs, refs = refs[5 : 5 + count], refs[5 + count :]
    if start_sweep:
        monitor_ref, balance_ref, pay_ref, acc_ref = refs
    else:
        det_ref, monitor_ref, balance_ref, pay_ref, acc_ref = refs
    rows, cols = monitor_ref.shape
    blocks = cols // TILE
    acc_ref[...] = jnp.zeros_like(acc_ref)
    add_sources(n_lon, partners, targets_ref, x_refs, near_ref, far_ref, acc_ref)

    field_id = lax.broadcasted_iota(jnp.int32, (FIELDS, TILE), 0)
    coef = jnp.zeros((FIELDS, TILE), jnp.float32)
    for f in range(FIELDS):
        coef = jnp.where(field_id == f, coef_ref[f], coef)
    for b in range(rows // 8):
        for c in range(blocks):
            parts = []
            for i in range(8):
                start = ((b * 8 + i) * blocks + c) * FIELDS
                place = slice(start, start + FIELDS)
                blended = moved_ref[place, :] + acc_ref[place, :]
                parts.append(coef * (blended * blended))
            monitor_ref[b * 8 : b * 8 + 8, c * TILE : (c + 1) * TILE] = jnp.sqrt(
                1.0 + sum_fields(parts)
            )

    monitor = monitor_ref[...]
    if start_sweep:
        det = jnp.ones((rows, cols), jnp.float32)
        balance = monitor
    else:
        det = det_ref[...]
        balance = monitor * det
    balance_ref[...] = balance
    inverse = 1.0 / monitor
    count = rows * cols
    mean = jnp.sum(jnp.sum(balance, axis=0, keepdims=True), axis=1, keepdims=True) / count
    away = balance - mean
    squares = jnp.sum(jnp.sum(away * away, axis=0, keepdims=True), axis=1, keepdims=True)
    lane_id = lax.broadcasted_iota(jnp.int32, (1, TILE), 1)
    stats = jnp.where(lane_id == 0, mean, jnp.where(lane_id == 1, squares, 0.0))
    stat_at = cols if start_sweep else 2 * cols
    for j in range(n_lat * n_lon):
        pay_ref[j, :, stat_at : stat_at + TILE] = stats

    lat, lon = mesh_place()
    left = lax.rem(lon + n_lon - 1, n_lon)
    right = lax.rem(lon + 1, n_lon)
    for side, col in ((left, 0), (right, cols - 1)):
        lanes = column_to_lanes(det[:, col : col + 1], 0)
        lanes = lanes + column_to_lanes(inverse[:, col : col + 1], rows)
        pay_ref[lat * n_lon + side, :, 0:TILE] = lanes

    def send_row(other, row):
        pay_ref[other * n_lon + lon, :, stat_at - cols : stat_at] = inverse[row : row + 1, :]
        if not start_sweep:
            pay_ref[other * n_lon + lon, :, 0:cols] = det[row : row + 1, :]
        for side, col in ((left, 0), (right, cols - 1)):
            lanes = jnp.where(
                lane_id == 0,
                det[row : row + 1, col : col + 1],
                inverse[row : row + 1, col : col + 1],
            )
            pay_ref[other * n_lon + side, :, 0:TILE] = lanes

    @pl.when(lat > 0)
    def _():
        send_row(lat - 1, 0)

    @pl.when(lat < n_lat - 1)
    def _():
        send_row(lat + 1, rows - 1)


def whole_stats(got_ref, n_dev, count, stat_at):
    total = got_ref[0, :, stat_at : stat_at + TILE]
    for j in range(1, n_dev):
        total = total + got_ref[j, :, stat_at : stat_at + TILE]
    target = lane_value(total, 0) / n_dev
    apart = jnp.zeros((1, TILE), jnp.float32)
    for j in range(n_dev):
        away = got_ref[j, :, stat_at : stat_at + TILE] - target
        apart = apart + away * away
    variance = (lane_value(total, 1) / count + lane_value(apart, 0)) / n_dev
    return target, jnp.sqrt(variance + 1e-06)


def update_kernel(n_lat, n_lon, n_got, *refs):
    place_ref = refs[0]
    got_refs = refs[1 : 1 + n_got]
    refs = refs[1 + n_got :]
    if n_got > 1:
        old_ref, refs = refs[0], refs[1:]
    monitor_ref, balance_ref, still_ref, lon_ref, lat_ref = refs[:5]
    pot_ref, det_ref, moved_ref = refs[5:8]
    send_refs, (zonal_ref, meridional_ref) = refs[8:-2], refs[-2:]
    rows, cols = monitor_ref.shape
    blocks = cols // TILE
    n_dev = n_lat * n_lon
    lat, lon = mesh_place()
    left = lax.rem(lon + n_lon - 1, n_lon)
    right = lax.rem(lon + 1, n_lon)
    below = jnp.maximum(lat - 1, 0)
    above = jnp.minimum(lat + 1, n_lat - 1)

    south_row = jnp.zeros((1, cols), jnp.float32)
    north_row = jnp.zeros((1, cols), jnp.float32)
    sides = [jnp.zeros((rows, 1), jnp.float32)] * 2
    corners = [jnp.zeros((1, 1), jnp.float32)] * 4
    for order, got_ref in enumerate(got_refs):
        stat_at = 2 * cols if order else cols
        target, spread = whole_stats(got_ref, n_dev, rows * cols, stat_at)

        def gain(det, inverse):
            return 0.5 * (det - target * inverse) / spread

        def row_from(j):
            det = got_ref[j, :, 0:cols] if stat_at > cols else 1.0
            return gain(det, got_ref[j, :, stat_at - cols : stat_at])

        south_row = south_row + row_from(below * n_lon + lon)
        north_row = north_row + row_from(above * n_lon + lon)
        for i, side in enumerate((left, right)):
            lanes = got_ref[lat * n_lon + side, :, 0:TILE]
            sides[i] = sides[i] + gain(
                lanes_to_column(lanes, rows, 0), lanes_to_column(lanes, rows, rows)
            )
        for i, (other, side) in enumerate(
            ((below, left), (below, right), (above, left), (above, right))
        ):
            lanes = got_ref[other * n_lon + side, :, 0:TILE]
            corners[i] = corners[i] + gain(lane_value(lanes, 0), lane_value(lanes, 1))

    has_south, has_north = lat > 0, lat < n_lat - 1
    south_row = jnp.where(has_south, south_row, 0.0)
    north_row = jnp.where(has_north, north_row, 0.0)
    corners = [
        jnp.where(has, corner, 0.0)
        for has, corner in zip((has_south, has_south, has_north, has_north), corners)
    ]

    potential = 0.5 * (balance_ref[...] - target) / (monitor_ref[...] * spread)
    if n_got > 1:
        potential = old_ref[...] + potential
    pot_ref[...] = potential

    row_id = lax.broadcasted_iota(jnp.int32, (rows, cols), 0)
    lane_id = lax.broadcasted_iota(jnp.int32, (rows, cols), 1)
    first, last = row_id == 0, row_id == rows - 1
    west_edge, east_edge = lane_id == 0, lane_id == cols - 1
    north = jnp.where(last, north_row, pltpu.roll(potential, rows - 1, 0))
    south = jnp.where(first, south_row, pltpu.roll(potential, 1, 0))
    east = jnp.where(east_edge, sides[1], pltpu.roll(potential, cols - 1, 1))
    west = jnp.where(west_edge, sides[0], pltpu.roll(potential, 1, 1))
    tall = north - south
    zonal_ref[...] = (east - west) * 0.5
    meridional_ref[...] = tall * 0.5

    for r in range(rows):
        for c in range(blocks):
            lanes = slice(c * TILE, (c + 1) * TILE)
            start = (r * blocks + c) * FIELDS
            place = slice(start, start + FIELDS)
            zonal = jnp.broadcast_to(zonal_ref[r : r + 1, lanes], (FIELDS, TILE))
            meridional = jnp.broadcast_to(meridional_ref[r : r + 1, lanes], (FIELDS, TILE))
            moved_ref[place, :] = (
                still_ref[place, :]
                + zonal * lon_ref[place, :]
                + meridional * lat_ref[place, :]
            )
    zero_tile(moved_ref)
    pack_tiles(lon, place_ref, moved_ref, send_refs)

    small_row = lax.broadcasted_iota(jnp.int32, (rows, TILE), 0)

    def side_tall(column, low, high):
        wide = jnp.broadcast_to(column, (rows, TILE))
        up = jnp.where(small_row == rows - 1, high, pltpu.roll(wide, rows - 1, 0))
        down = jnp.where(small_row == 0, low, pltpu.roll(wide, 1, 0))
        return (up - down)[:, 0:1]

    west_tall = side_tall(sides[0], corners[0], corners[2])
    east_tall = side_tall(sides[1], corners[1], corners[3])
    tall_east = jnp.where(east_edge, east_tall, pltpu.roll(tall, cols - 1, 1))
    tall_west = jnp.where(west_edge, west_tall, pltpu.roll(tall, 1, 1))
    mixed = (tall_east - tall_west) * 0.25
    second_lon = east - 2.0 * potential + west
    second_lat = north - 2.0 * potential + south
    det_ref[...] = (1.0 + second_lon) * (1.0 + second_lat) - mixed * mixed


def last_kernel(n_dev, got_ref, old_ref, monitor_ref, balance_ref, pot_ref, scaled_ref):
    rows, cols = monitor_ref.shape
    target, spread = whole_stats(got_ref, n_dev, rows * cols, 0)
    residual = balance_ref[...] - target
    scaled_ref[...] = residual / spread
    pot_ref[...] = old_ref[...] + 0.5 * residual / (monitor_ref[...] * spread)


def per_device(pq, coef, departing, occupancy, arriving, blocks_w):
    n_lat, n_lon = lax.axis_size("lat"), lax.axis_size("lon")
    n_dev = n_lat * n_lon
    rows, cols = pq.shape[2:]
    ids = departing[0, 0]
    occ = occupancy[0, 0]
    targets = arriving[0, 0]
    weights = blocks_w[0, 0]
    smem = pl.BlockSpec(memory_space=SMEM)
    vmem = pl.BlockSpec(memory_space=VMEM)
    hbm = pl.BlockSpec(memory_space=pltpu.MemorySpace.HBM)
    f32 = jnp.float32
    grid = jax.ShapeDtypeStruct((rows, cols), f32)
    half = n_lon // 2
    tile_rows = FIELDS * rows * cols // TILE
    acc_shape = jax.ShapeDtypeStruct((tile_rows, TILE), f32)
    moved_shape = jax.ShapeDtypeStruct((tile_rows + FIELDS, TILE), f32)
    send_shape = jax.ShapeDtypeStruct((CAP * FIELDS, TILE), jnp.bfloat16)
    half_shape = VMEM((half, CAP, TILE, TILE), weights.dtype)
    params = pltpu.CompilerParams(vmem_limit_bytes=5 << 20)
    early_cost = pl.CostEstimate(
        flops=2 * half * CAP * FIELDS * TILE * TILE,
        bytes_accessed=2 * half * CAP * TILE * TILE,
        transcendentals=0,
    )

    def in_hbm(array):
        return pltpu.with_memory_space_constraint(array, pltpu.MemorySpace.HBM)

    still, places, targets, coef, *send = pl.pallas_call(
        functools.partial(first_kernel, n_lon),
        out_shape=(
            moved_shape,
            jax.ShapeDtypeStruct(ids.shape, ids.dtype),
            jax.ShapeDtypeStruct(targets.shape, targets.dtype),
            jax.ShapeDtypeStruct(coef.shape, coef.dtype),
        )
        + (send_shape,) * n_lon,
        in_specs=[hbm] * 5,
        out_specs=(vmem,) * (4 + n_lon),
        scratch_shapes=[
            pltpu.VMEM(ids.shape, jnp.int32),
            pltpu.SMEM(occ.shape, jnp.int32),
            pltpu.SMEM(ids.shape, jnp.int32),
            pltpu.VMEM(pq.shape[1:], pq.dtype),
            pltpu.SemaphoreType.DMA((5,)),
        ],
        compiler_params=params,
        name="first",
    )(*[in_hbm(x) for x in (ids, occ, targets, coef, pq)])

    def interp(send, moved, det, kept):
        got = list(send)
        for r in range(1, n_lon):
            got[r] = lax.ppermute(send[r], "lon", [(i, i ^ r) for i in range(n_lon)])
        early, late = ([got[r] for r in group] for group in groups(n_lon))
        start_sweep = det is None
        if start_sweep:
            args = [in_hbm(pq), in_hbm(weights)]
            out_shape = (acc_shape, half_shape, half_shape, acc_shape, acc_shape)
            scratch = [
                pltpu.VMEM((2,) + pq.shape[1:], pq.dtype),
                pltpu.SemaphoreType.DMA((3,)),
            ]
        else:
            args, out_shape, scratch = list(kept[:2]), (acc_shape,), []
        base, *fetched = pl.pallas_call(
            functools.partial(early_kernel, n_lon, start_sweep),
            out_shape=out_shape,
            in_specs=[smem]
            + [vmem] * (1 + len(early))
            + [hbm if start_sweep else vmem] * len(args),
            out_specs=(vmem,) * len(out_shape),
            scratch_shapes=scratch,
            compiler_params=params,
            cost_estimate=early_cost,
            name="early",
        )(targets, moved, *early, *args)
        kept = fetched if start_sweep else kept
        pay_width = TILE + (cols if start_sweep else 2 * cols)
        out_shape = (grid, grid, jax.ShapeDtypeStruct((n_dev, 1, pay_width), f32))
        args = [targets, coef, base, *kept[:2], *late] + ([] if start_sweep else [det])
        outs = pl.pallas_call(
            functools.partial(late_kernel, n_lat, n_lon, start_sweep),
            out_shape=out_shape,
            in_specs=[smem, smem] + [vmem] * (len(args) - 2),
            out_specs=(vmem,) * 3,
            scratch_shapes=[pltpu.VMEM((tile_rows, TILE), f32)],
            compiler_params=params,
            name="late",
        )(*args)
        return (*outs, kept)

    def share(pay):
        return lax.all_to_all(pay, ("lat", "lon"), 0, 0, tiled=True)

    gots = []
    moved = still
    potential = det = kept = None
    for sweep in range(SWEEPS):
        monitor, balance, pay, kept = interp(send, moved, det, kept)
        if sweep == SWEEPS - 1:
            break
        gots.append(share(pay))
        olds = [] if potential is None else [potential]
        args = [places, *gots, *olds, monitor, balance, still, *kept[2:]]
        potential, det, moved, *send = pl.pallas_call(
            functools.partial(update_kernel, n_lat, n_lon, len(gots)),
            out_shape=(grid, grid, moved_shape) + (send_shape,) * n_lon,
            in_specs=[smem] + [vmem] * (len(args) - 1),
            out_specs=(vmem,) * (3 + n_lon),
            scratch_shapes=[pltpu.VMEM((rows, cols), f32)] * 2,
            compiler_params=params,
            name="update",
        )(*args)

    got = share(pay[:, :, pay.shape[2] - TILE :])
    return pl.pallas_call(
        functools.partial(last_kernel, n_dev),
        out_shape=(grid, grid),
        in_specs=[vmem] * 4,
        out_specs=(vmem, vmem),
        compiler_params=params,
        name="last",
    )(got, potential, monitor, balance)


def solution(mesh):
    in_specs = (
        P(None, None, "lat", "lon"),
        P(),
        P("lat", "lon", None, None),
        P("lat", "lon", None),
        P("lat", "lon", None, None),
        P("lat", "lon", None, None, None, None),
    )
    out_specs = (P("lat", "lon"), P("lat", "lon"))
    return jax.shard_map(
        per_device, mesh=mesh, in_specs=in_specs, out_specs=out_specs, check_vma=False
    )
```

profile of v0, /device:TPU:0, one launch (start us, length us, event | category | flops | bytes accessed | tf_op | source)
XLA Modules:
  0.0 91.7 jit_solution(6574234897054118303)
XLA Ops:
  0.6 1.7 %first.1 = (f32[2056,128]{1,0:T(8,128)S(1)}, s32[8,32]{1,0:T(8,128)S(1)}, s32[8,32]{1,0:T(8,128)S(1)}, f32[8]{0:T(128)S(1)}, bf16[256,128]{1,0:T(8,128)(2,1)S(1)...) custom-call(s32[8,32]{1,0:T(8,128)} %bitcast.5, ...), custom_call_target="tpu_custom_call" | custom-call | tf_op jit(solution)/shard_map/first/pallas_call | solution.py:415
  2.9 4.7 %collective-permute-start.1 = (bf16[256,128]{1,0:T(8,128)(2,1)S(1)}, bf16[256,128]{1,0:T(8,128)(2,1)S(1)}, u32[]{:S(2)}, u32[]{:S(2)}) collective-permute-start(bf16[256,128]{1,0:T(8,128)(2,1)S(1)} %get-tuple-element.56), channel_id=1, source_target_pairs={{0,7},{1,6},{2,5},{3,4},{4,3},{5,2},{6,1},{7,0},{8,15},{9,14},{10,... | collective-permute-start | bytes 196616 | tf_op jit(solution)/shard_map/ppermute | solution.py:440
  7.6 1.4 %collective-permute-start.4 = (bf16[256,128]{1,0:T(8,128)(2,1)S(1)}, bf16[256,128]{1,0:T(8,128)(2,1)S(1)}, u32[]{:S(2)}, u32[]{:S(2)}) collective-permute-start(bf16[256,128]{1,0:T(8,128)(2,1)S(1)} %get-tuple-element.62), channel_id=1, source_target_pairs={{0,3},{1,2},{2,1},{3,0},{4,7},{5,6},{6,5},{7,4},{8,11},{9,10},{10,... | collective-permute-start | bytes 196616 | tf_op jit(solution)/shard_map/ppermute | solution.py:440
  9.0 2.9 %collective-permute-start.5 = (bf16[256,128]{1,0:T(8,128)(2,1)S(1)}, bf16[256,128]{1,0:T(8,128)(2,1)S(1)}, u32[]{:S(2)}, u32[]{:S(2)}) collective-permute-start(bf16[256,128]{1,0:T(8,128)(2,1)S(1)} %get-tuple-element.63), channel_id=1, source_target_pairs={{0,4},{1,5},{2,6},{3,7},{4,0},{5,1},{6,2},{7,3},{8,12},{9,13},{10,... | collective-permute-start | bytes 196616 | tf_op jit(solution)/shard_map/ppermute | solution.py:440
  12.0 2.1 %collective-permute-done.2.refs_5_ = bf16[256,128]{1,0:T(8,128)(2,1)S(1)} collective-permute-done((bf16[256,128]{1,0:T(8,128)(2,1)S(1)}, bf16[256,128]{1,0:T(8,128)(2,1)S(1)}, u32[]{:S(2)}, u32[]{:S(2)}) %collective-permute-start.2) | collective-permute-done | bytes 65568 | tf_op jit(solution)/shard_map/ppermute | solution.py:440
  14.2 5.2 %early.3 = (f32[2048,128]{1,0:T(8,128)S(1)}, bf16[4,32,128,128]{3,2,1,0:T(8,128)(2,1)S(1)}, bf16[4,32,128,128]{3,2,1,0:T(8,128)(2,1)S(1)}, f32[2048,128]{1,0:T(8,128)S(1)}, f32[2048,128]{1,0:T(8,128)S(1)}) custom-call(s32[8,32]{1,0:T(8,128)S(1)} %get-tuple-element.50.refs_0_, f32[2056,128]{1,0:T(8,128)S(1)} %get-tuple-element.53.refs_1_.refs_4_.refs_6_, ...), custom_call_target="tpu_custom_call" | custom-call | flops 33554432 | bytes 4194304 | tf_op jit(solution)/shard_map/early/pallas_call | solution.py:452
  20.0 1.9 %late.3 = (f32[64,512]{1,0:T(8,128)S(1)}, f32[64,512]{1,0:T(8,128)S(1)}, f32[32,1,640]{2,1,0:T(1,128)S(1)}) custom-call(s32[8,32]{1,0:T(8,128)S(1)} %get-tuple-element.50.refs_0_, f32[8]{0:T(128)S(1)} %get-tuple-element.51.refs_1_, f32[2048,128]{1,0:T(8,128)S(1)} %get-tuple-element.58.refs_2_, ...), custom_call_target="tpu_custom_call" | custom-call | tf_op jit(solution)/shard_map/late/pallas_call | solution.py:468
  21.9 12.2 %all_to_all.15.refs_1_ = f32[32,1,640]{2,1,0:T(1,128)S(1)} all-to-all(f32[32,1,640]{2,1,0:T(1,128)S(1)} %get-tuple-element.65), channel_id=1, replica_groups=mesh['lat'=4,'lon'=8] {'lat','lon'}, dimensions={0} | all-to-all | bytes 163840 | tf_op jit(solution)/shard_map/all_to_all | solution.py:480
  34.1 1.6 %update.2 = (f32[64,512]{1,0:T(8,128)S(1)}, f32[64,512]{1,0:T(8,128)S(1)}, f32[2056,128]{1,0:T(8,128)S(1)}, bf16[256,128]{1,0:T(8,128)(2,1)S(1)}, bf16[256,128]{...) custom-call(s32[8,32]{1,0:T(8,128)S(1)} %get-tuple-element.52.refs_0, ...), custom_call_target="tpu_custom_call" | custom-call | tf_op jit(solution)/shard_map/update/pallas_call | solution.py:492
  36.7 3.0 %collective-permute-start.9 = (bf16[256,128]{1,0:T(8,128)(2,1)S(1)}, bf16[256,128]{1,0:T(8,128)(2,1)S(1)}, u32[]{:S(2)}, u32[]{:S(2)}) collective-permute-start(bf16[256,128]{1,0:T(8,128)(2,1)S(1)} %get-tuple-element.74), channel_id=1, source_target_pairs={{0,6},{1,7},{2,4},{3,5},{4,2},{5,3},{6,0},{7,1},{8,14},{9,15},{10,... | collective-permute-start | bytes 196616 | tf_op jit(solution)/shard_map/ppermute | solution.py:440
  41.6 2.5 %collective-permute-start.13 = (bf16[256,128]{1,0:T(8,128)(2,1)S(1)}, bf16[256,128]{1,0:T(8,128)(2,1)S(1)}, u32[]{:S(2)}, u32[]{:S(2)}) collective-permute-start(bf16[256,128]{1,0:T(8,128)(2,1)S(1)} %get-tuple-element.78), channel_id=1, source_target_pairs={{0,5},{1,4},{2,7},{3,6},{4,1},{5,0},{6,3},{7,2},{8,13},{9,12},{10,... | collective-permute-start | bytes 196616 | tf_op jit(solution)/shard_map/ppermute | solution.py:440
  44.1 1.4 %early.4.refs_2_ = f32[2048,128]{1,0:T(8,128)S(1)} custom-call(s32[8,32]{1,0:T(8,128)S(1)} %get-tuple-element.50.refs_0_, f32[2056,128]{1,0:T(8,128)S(1)} %get-tuple-element.70.refs_1_, bf16[256,128]{1,0:T(8,128)(2,1)S(1)} %get-tuple-element.71.refs_2_, bf16[256,128]{1,0:T(8,128)(2,1)S(1)} %collective-permute-done.7.refs_3_, ...), custom_call_target="tpu_custom_call" | custom-call | flops 33554432 | bytes 4194304 | tf_op jit(solution)/shard_map/early/pallas_call | solution.py:452
  45.5 1.9 %collective-permute-done.11.refs_6_ = bf16[256,128]{1,0:T(8,128)(2,1)S(1)} collective-permute-done((bf16[256,128]{1,0:T(8,128)(2,1)S(1)}, bf16[256,128]{1,0:T(8,128)(2,1)S(1)}, u32[]{:S(2)}, u32[]{:S(2)}) %collective-permute-start.11) | collective-permute-done | bytes 65568 | tf_op jit(solution)/shard_map/ppermute | solution.py:440
  47.4 2.2 %collective-permute-done.12.refs_7_ = bf16[256,128]{1,0:T(8,128)(2,1)S(1)} collective-permute-done((bf16[256,128]{1,0:T(8,128)(2,1)S(1)}, bf16[256,128]{1,0:T(8,128)(2,1)S(1)}, u32[]{:S(2)}, u32[]{:S(2)}) %collective-permute-start.12) | collective-permute-done | bytes 65568 | tf_op jit(solution)/shard_map/ppermute | solution.py:440
  50.9 1.9 %late.4 = (f32[64,512]{1,0:T(8,128)S(1)}, f32[64,512]{1,0:T(8,128)S(1)}, f32[32,1,1152]{2,1,0:T(1,128)S(1)}) custom-call(s32[8,32]{1,0:T(8,128)S(1)} %get-tuple-element.50.refs_0_, f32[8]{0:T(128)S(1)} %get-tuple-element.51.refs_1_, f32[2048,128]{1,0:T(8,128)S(1)} %early.4.refs_2_, bf16[4,32,128,128]{3,2,1,0:T(8,128)(2,1)S(1)} %get-tuple-element.59.refs_3_.refs_6_, ...), custom_call_target="tpu_custom_call" | custom-call | tf_op jit(solution)/shard_map/late/pallas_call | solution.py:468
  52.8 10.1 %all_to_all.16.refs_2_ = f32[32,1,1152]{2,1,0:T(1,128)S(1)} all-to-all(f32[32,1,1152]{2,1,0:T(1,128)S(1)} %get-tuple-element.80), channel_id=1, replica_groups=mesh['lat'=4,'lon'=8] {'lat','lon'}, dimensions={0} | all-to-all | bytes 294912 | tf_op jit(solution)/shard_map/all_to_all | solution.py:480
  62.9 1.6 %update.3 = (f32[64,512]{1,0:T(8,128)S(1)}, f32[64,512]{1,0:T(8,128)S(1)}, f32[2056,128]{1,0:T(8,128)S(1)}, bf16[256,128]{1,0:T(8,128)(2,1)S(1)}, bf16[256,128]{...) custom-call(s32[8,32]{1,0:T(8,128)S(1)} %get-tuple-element.52.refs_0, ...), custom_call_target="tpu_custom_call" | custom-call | tf_op jit(solution)/shard_map/update/pallas_call | solution.py:492
  65.7 2.9 %collective-permute-start.16 = (bf16[256,128]{1,0:T(8,128)(2,1)S(1)}, bf16[256,128]{1,0:T(8,128)(2,1)S(1)}, u32[]{:S(2)}, u32[]{:S(2)}) collective-permute-start(bf16[256,128]{1,0:T(8,128)(2,1)S(1)} %get-tuple-element.88), channel_id=1, source_target_pairs={{0,6},{1,7},{2,4},{3,5},{4,2},{5,3},{6,0},{7,1},{8,14},{9,15},{10,... | collective-permute-start | bytes 196616 | tf_op jit(solution)/shard_map/ppermute | solution.py:440
  68.6 1.4 %collective-permute-start.18 = (bf16[256,128]{1,0:T(8,128)(2,1)S(1)}, bf16[256,128]{1,0:T(8,128)(2,1)S(1)}, u32[]{:S(2)}, u32[]{:S(2)}) collective-permute-start(bf16[256,128]{1,0:T(8,128)(2,1)S(1)} %get-tuple-element.90), channel_id=1, source_target_pairs={{0,3},{1,2},{2,1},{3,0},{4,7},{5,6},{6,5},{7,4},{8,11},{9,10},{10,... | collective-permute-start | bytes 196616 | tf_op jit(solution)/shard_map/ppermute | solution.py:440
  70.9 2.0 %collective-permute-start.20 = (bf16[256,128]{1,0:T(8,128)(2,1)S(1)}, bf16[256,128]{1,0:T(8,128)(2,1)S(1)}, u32[]{:S(2)}, u32[]{:S(2)}) collective-permute-start(bf16[256,128]{1,0:T(8,128)(2,1)S(1)} %get-tuple-element.92), channel_id=1, source_target_pairs={{0,5},{1,4},{2,7},{3,6},{4,1},{5,0},{6,3},{7,2},{8,13},{9,12},{10,... | collective-permute-start | bytes 196616 | tf_op jit(solution)/shard_map/ppermute | solution.py:440
  74.4 2.4 %collective-permute-done.18.refs_6_ = bf16[256,128]{1,0:T(8,128)(2,1)S(1)} collective-permute-done((bf16[256,128]{1,0:T(8,128)(2,1)S(1)}, bf16[256,128]{1,0:T(8,128)(2,1)S(1)}, u32[]{:S(2)}, u32[]{:S(2)}) %collective-permute-start.18) | collective-permute-done | bytes 65568 | tf_op jit(solution)/shard_map/ppermute | solution.py:440
  76.7 1.9 %collective-permute-done.19.refs_7_ = bf16[256,128]{1,0:T(8,128)(2,1)S(1)} collective-permute-done((bf16[256,128]{1,0:T(8,128)(2,1)S(1)}, bf16[256,128]{1,0:T(8,128)(2,1)S(1)}, u32[]{:S(2)}, u32[]{:S(2)}) %collective-permute-start.19) | collective-permute-done | bytes 65568 | tf_op jit(solution)/shard_map/ppermute | solution.py:440
  79.6 1.9 %late.5 = (f32[64,512]{1,0:T(8,128)S(1)}, f32[64,512]{1,0:T(8,128)S(1)}, f32[32,1,1152]{2,1,0:T(1,128)S(1)}) custom-call(s32[8,32]{1,0:T(8,128)S(1)} %get-tuple-element.50.refs_0_, f32[8]{0:T(128)S(1)} %get-tuple-element.51.refs_1_, f32[2048,128]{1,0:T(8,128)S(1)} %early.5.refs_2_, bf16[4,32,128,128]{3,2,1,0:T(8,128)(2,1)S(1)} %get-tuple-element.59.refs_3_.refs_6_, ...), custom_call_target="tpu_custom_call" | custom-call | tf_op jit(solution)/shard_map/late/pallas_call | solution.py:468
  81.5 9.2 %all_to_all.17.got_ref = f32[32,1,128]{2,1,0:T(1,128)S(1)} all-to-all(f32[32,1,128]{2,1,0:T(1,128)S(1)} %slice.3), channel_id=1, replica_groups=mesh['lat'=4,'lon'=8] {'lat','lon'}, dimensions={0} | all-to-all | bytes 32768 | tf_op jit(solution)/shard_map/all_to_all | solution.py:480
  (32 shorter events, 10.9 us)
Async XLA Ops:
  2.3 6.7 %collective-permute-start = (bf16[256,128]{1,0:T(8,128)(2,1)S(1)}, bf16[256,128]{1,0:T(8,128)(2,1)S(1)}, u32[]{:S(2)}, u32[]{:S(2)}) collective-permute-start(bf16[256,128]{1,0:T(8,128)(2,1)S(1)} %get-tuple-element.55), channel_id=1, source_target_pairs={{0,1},{1,0},{2,3},{3,2},{4,5},{5,4},{6,7},{7,6},{8,9},{9,8},{10,11... | collective-permute-start | bytes 196616 | tf_op jit(solution)/shard_map/ppermute | solution.py:440
  2.9 9.1 %collective-permute-start.1 = (bf16[256,128]{1,0:T(8,128)(2,1)S(1)}, bf16[256,128]{1,0:T(8,128)(2,1)S(1)}, u32[]{:S(2)}, u32[]{:S(2)}) collective-permute-start(bf16[256,128]{1,0:T(8,128)(2,1)S(1)} %get-tuple-element.56), channel_id=1, source_target_pairs={{0,7},{1,6},{2,5},{3,4},{4,3},{5,2},{6,1},{7,0},{8,15},{9,14},{10,... | collective-permute-start | bytes 196616 | tf_op jit(solution)/shard_map/ppermute | solution.py:440
  7.6 6.6 %collective-permute-start.2 = (bf16[256,128]{1,0:T(8,128)(2,1)S(1)}, bf16[256,128]{1,0:T(8,128)(2,1)S(1)}, u32[]{:S(2)}, u32[]{:S(2)}) collective-permute-start(bf16[256,128]{1,0:T(8,128)(2,1)S(1)} %get-tuple-element.57), channel_id=1, source_target_pairs={{0,6},{1,7},{2,4},{3,5},{4,2},{5,3},{6,0},{7,1},{8,14},{9,15},{10,... | collective-permute-start | bytes 196616 | tf_op jit(solution)/shard_map/ppermute | solution.py:440
  7.6 11.7 %collective-permute-start.3 = (bf16[256,128]{1,0:T(8,128)(2,1)S(1)}, bf16[256,128]{1,0:T(8,128)(2,1)S(1)}, u32[]{:S(2)}, u32[]{:S(2)}) collective-permute-start(bf16[256,128]{1,0:T(8,128)(2,1)S(1)} %get-tuple-element.61), channel_id=1, source_target_pairs={{0,2},{1,3},{2,0},{3,1},{4,6},{5,7},{6,4},{7,5},{8,10},{9,11},{10,... | collective-permute-start | bytes 196616 | tf_op jit(solution)/shard_map/ppermute | solution.py:440
  7.6 11.7 %collective-permute-start.4 = (bf16[256,128]{1,0:T(8,128)(2,1)S(1)}, bf16[256,128]{1,0:T(8,128)(2,1)S(1)}, u32[]{:S(2)}, u32[]{:S(2)}) collective-permute-start(bf16[256,128]{1,0:T(8,128)(2,1)S(1)} %get-tuple-element.62), channel_id=1, source_target_pairs={{0,3},{1,2},{2,1},{3,0},{4,7},{5,6},{6,5},{7,4},{8,11},{9,10},{10,... | collective-permute-start | bytes 196616 | tf_op jit(solution)/shard_map/ppermute | solution.py:440
  9.0 10.3 %collective-permute-start.5 = (bf16[256,128]{1,0:T(8,128)(2,1)S(1)}, bf16[256,128]{1,0:T(8,128)(2,1)S(1)}, u32[]{:S(2)}, u32[]{:S(2)}) collective-permute-start(bf16[256,128]{1,0:T(8,128)(2,1)S(1)} %get-tuple-element.63), channel_id=1, source_target_pairs={{0,4},{1,5},{2,6},{3,7},{4,0},{5,1},{6,2},{7,3},{8,12},{9,13},{10,... | collective-permute-start | bytes 196616 | tf_op jit(solution)/shard_map/ppermute | solution.py:440
  12.0 8.1 %collective-permute-start.6 = (bf16[256,128]{1,0:T(8,128)(2,1)S(1)}, bf16[256,128]{1,0:T(8,128)(2,1)S(1)}, u32[]{:S(2)}, u32[]{:S(2)}) collective-permute-start(bf16[256,128]{1,0:T(8,128)(2,1)S(1)} %get-tuple-element.64), channel_id=1, source_target_pairs={{0,5},{1,4},{2,7},{3,6},{4,1},{5,0},{6,3},{7,2},{8,13},{9,12},{10,... | collective-permute-start | bytes 196616 | tf_op jit(solution)/shard_map/ppermute | solution.py:440
  35.7 5.2 %collective-permute-start.7 = (bf16[256,128]{1,0:T(8,128)(2,1)S(1)}, bf16[256,128]{1,0:T(8,128)(2,1)S(1)}, u32[]{:S(2)}, u32[]{:S(2)}) collective-permute-start(bf16[256,128]{1,0:T(8,128)(2,1)S(1)} %get-tuple-element.72), channel_id=1, source_target_pairs={{0,1},{1,0},{2,3},{3,2},{4,5},{5,4},{6,7},{7,6},{8,9},{9,8},{10,11... | collective-permute-start | bytes 196616 | tf_op jit(solution)/shard_map/ppermute | solution.py:440
  35.9 5.7 %collective-permute-start.8 = (bf16[256,128]{1,0:T(8,128)(2,1)S(1)}, bf16[256,128]{1,0:T(8,128)(2,1)S(1)}, u32[]{:S(2)}, u32[]{:S(2)}) collective-permute-start(bf16[256,128]{1,0:T(8,128)(2,1)S(1)} %get-tuple-element.73), channel_id=1, source_target_pairs={{0,7},{1,6},{2,5},{3,4},{4,3},{5,2},{6,1},{7,0},{8,15},{9,14},{10,... | collective-permute-start | bytes 196616 | tf_op jit(solution)/shard_map/ppermute | solution.py:440
  36.7 7.4 %collective-permute-start.9 = (bf16[256,128]{1,0:T(8,128)(2,1)S(1)}, bf16[256,128]{1,0:T(8,128)(2,1)S(1)}, u32[]{:S(2)}, u32[]{:S(2)}) collective-permute-start(bf16[256,128]{1,0:T(8,128)(2,1)S(1)} %get-tuple-element.74), channel_id=1, source_target_pairs={{0,6},{1,7},{2,4},{3,5},{4,2},{5,3},{6,0},{7,1},{8,14},{9,15},{10,... | collective-permute-start | bytes 196616 | tf_op jit(solution)/shard_map/ppermute | solution.py:440
  39.7 5.8 %collective-permute-start.10 = (bf16[256,128]{1,0:T(8,128)(2,1)S(1)}, bf16[256,128]{1,0:T(8,128)(2,1)S(1)}, u32[]{:S(2)}, u32[]{:S(2)}) collective-permute-start(bf16[256,128]{1,0:T(8,128)(2,1)S(1)} %get-tuple-element.75), channel_id=1, source_target_pairs={{0,2},{1,3},{2,0},{3,1},{4,6},{5,7},{6,4},{7,5},{8,10},{9,11},{10,... | collective-permute-start | bytes 196616 | tf_op jit(solution)/shard_map/ppermute | solution.py:440
  39.7 7.7 %collective-permute-start.11 = (bf16[256,128]{1,0:T(8,128)(2,1)S(1)}, bf16[256,128]{1,0:T(8,128)(2,1)S(1)}, u32[]{:S(2)}, u32[]{:S(2)}) collective-permute-start(bf16[256,128]{1,0:T(8,128)(2,1)S(1)} %get-tuple-element.76), channel_id=1, source_target_pairs={{0,3},{1,2},{2,1},{3,0},{4,7},{5,6},{6,5},{7,4},{8,11},{9,10},{10,... | collective-permute-start | bytes 196616 | tf_op jit(solution)/shard_map/ppermute | solution.py:440
  40.9 8.7 %collective-permute-start.12 = (bf16[256,128]{1,0:T(8,128)(2,1)S(1)}, bf16[256,128]{1,0:T(8,128)(2,1)S(1)}, u32[]{:S(2)}, u32[]{:S(2)}) collective-permute-start(bf16[256,128]{1,0:T(8,128)(2,1)S(1)} %get-tuple-element.77), channel_id=1, source_target_pairs={{0,4},{1,5},{2,6},{3,7},{4,0},{5,1},{6,2},{7,3},{8,12},{9,13},{10,... | collective-permute-start | bytes 196616 | tf_op jit(solution)/shard_map/ppermute | solution.py:440
  41.6 9.3 %collective-permute-start.13 = (bf16[256,128]{1,0:T(8,128)(2,1)S(1)}, bf16[256,128]{1,0:T(8,128)(2,1)S(1)}, u32[]{:S(2)}, u32[]{:S(2)}) collective-permute-start(bf16[256,128]{1,0:T(8,128)(2,1)S(1)} %get-tuple-element.78), channel_id=1, source_target_pairs={{0,5},{1,4},{2,7},{3,6},{4,1},{5,0},{6,3},{7,2},{8,13},{9,12},{10,... | collective-permute-start | bytes 196616 | tf_op jit(solution)/shard_map/ppermute | solution.py:440
  64.6 5.4 %collective-permute-start.14 = (bf16[256,128]{1,0:T(8,128)(2,1)S(1)}, bf16[256,128]{1,0:T(8,128)(2,1)S(1)}, u32[]{:S(2)}, u32[]{:S(2)}) collective-permute-start(bf16[256,128]{1,0:T(8,128)(2,1)S(1)} %get-tuple-element.86), channel_id=1, source_target_pairs={{0,1},{1,0},{2,3},{3,2},{4,5},{5,4},{6,7},{7,6},{8,9},{9,8},{10,11... | collective-permute-start | bytes 196616 | tf_op jit(solution)/shard_map/ppermute | solution.py:440
  65.0 6.0 %collective-permute-start.15 = (bf16[256,128]{1,0:T(8,128)(2,1)S(1)}, bf16[256,128]{1,0:T(8,128)(2,1)S(1)}, u32[]{:S(2)}, u32[]{:S(2)}) collective-permute-start(bf16[256,128]{1,0:T(8,128)(2,1)S(1)} %get-tuple-element.87), channel_id=1, source_target_pairs={{0,7},{1,6},{2,5},{3,4},{4,3},{5,2},{6,1},{7,0},{8,15},{9,14},{10,... | collective-permute-start | bytes 196616 | tf_op jit(solution)/shard_map/ppermute | solution.py:440
  65.7 7.3 %collective-permute-start.16 = (bf16[256,128]{1,0:T(8,128)(2,1)S(1)}, bf16[256,128]{1,0:T(8,128)(2,1)S(1)}, u32[]{:S(2)}, u32[]{:S(2)}) collective-permute-start(bf16[256,128]{1,0:T(8,128)(2,1)S(1)} %get-tuple-element.88), channel_id=1, source_target_pairs={{0,6},{1,7},{2,4},{3,5},{4,2},{5,3},{6,0},{7,1},{8,14},{9,15},{10,... | collective-permute-start | bytes 196616 | tf_op jit(solution)/shard_map/ppermute | solution.py:440
  68.6 5.8 %collective-permute-start.17 = (bf16[256,128]{1,0:T(8,128)(2,1)S(1)}, bf16[256,128]{1,0:T(8,128)(2,1)S(1)}, u32[]{:S(2)}, u32[]{:S(2)}) collective-permute-start(bf16[256,128]{1,0:T(8,128)(2,1)S(1)} %get-tuple-element.89), channel_id=1, source_target_pairs={{0,2},{1,3},{2,0},{3,1},{4,6},{5,7},{6,4},{7,5},{8,10},{9,11},{10,... | collective-permute-start | bytes 196616 | tf_op jit(solution)/shard_map/ppermute | solution.py:440
  68.6 8.2 %collective-permute-start.18 = (bf16[256,128]{1,0:T(8,128)(2,1)S(1)}, bf16[256,128]{1,0:T(8,128)(2,1)S(1)}, u32[]{:S(2)}, u32[]{:S(2)}) collective-permute-start(bf16[256,128]{1,0:T(8,128)(2,1)S(1)} %get-tuple-element.90), channel_id=1, source_target_pairs={{0,3},{1,2},{2,1},{3,0},{4,7},{5,6},{6,5},{7,4},{8,11},{9,10},{10,... | collective-permute-start | bytes 196616 | tf_op jit(solution)/shard_map/ppermute | solution.py:440
  70.0 8.7 %collective-permute-start.19 = (bf16[256,128]{1,0:T(8,128)(2,1)S(1)}, bf16[256,128]{1,0:T(8,128)(2,1)S(1)}, u32[]{:S(2)}, u32[]{:S(2)}) collective-permute-start(bf16[256,128]{1,0:T(8,128)(2,1)S(1)} %get-tuple-element.91), channel_id=1, source_target_pairs={{0,4},{1,5},{2,6},{3,7},{4,0},{5,1},{6,2},{7,3},{8,12},{9,13},{10,... | collective-permute-start | bytes 196616 | tf_op jit(solution)/shard_map/ppermute | solution.py:440
  70.9 8.6 %collective-permute-start.20 = (bf16[256,128]{1,0:T(8,128)(2,1)S(1)}, bf16[256,128]{1,0:T(8,128)(2,1)S(1)}, u32[]{:S(2)}, u32[]{:S(2)}) collective-permute-start(bf16[256,128]{1,0:T(8,128)(2,1)S(1)} %get-tuple-element.92), channel_id=1, source_target_pairs={{0,5},{1,4},{2,7},{3,6},{4,1},{5,0},{6,3},{7,2},{8,13},{9,12},{10,... | collective-permute-start | bytes 196616 | tf_op jit(solution)/shard_map/ppermute | solution.py:440
where the time goes:
time: 91.9 us; the launch traced here: 91.7 us
  blocking collectives  31.5 us (34%)
  starting transfers between devices  25.1 us (27%)
  Pallas kernels  19.4 us (21%)
  waiting for transfers between devices  14.8 us (16%)
    all_to_all x3, blocking collectives, share(): return lax.all_to_all(pay, ('lat', 'lon'), 0, 0, tiled=True)  31.5 us
    ppermute x21, starting transfers between devices, interp(): got[r] = lax.ppermute(send[r], 'lon', [(i, i ^ r) for i in range(n_lon)])  25.1 us
    ppermute x21, waiting for transfers between devices, interp(): got[r] = lax.ppermute(send[r], 'lon', [(i, i ^ r) for i in range(n_lon)])  14.8 us
    pallas_call x3, Pallas kernels, interp(): pl.pallas_call(functools.partial(early_kernel, n_lon, start_sweep), out_s...  7.93 us
    pallas_call x3, Pallas kernels, interp(): pl.pallas_call(functools.partial(late_kernel, n_lat, n_lon, start_sweep),...  5.64 us
    pallas_call x2, Pallas kernels, per_device(): pl.pallas_call(functools.partial(update_kernel, n_lat, n_lon, len(gots)),...  3.25 us
  transfers between devices with their start and end apart: 21, of which 10 were waited for; matrix products, arithmetic and copies ran while one was open for 0% of the time, Pallas kernels for 9%

commit v1 on v0

--- a/solution.py
+++ b/solution.py
@@ -155,35 +155,33 @@
         add_source(lon ^ r, (lon ^ r) & (half - 1), targets_ref, x_ref, w_ref, acc_ref)
 
 
-def early_kernel(n_lon, start_sweep, *refs):
+def fetch_kernel(n_lon, *refs):
+    pq_hbm, w_hbm, near_ref, far_ref, lon_ref, lat_ref, pq_ref, sems = refs
     half = n_lon // 2
-    partners = groups(n_lon)[0]
-    count = len(partners)
-    targets_ref, moved_ref, x_refs, refs = refs[0], refs[1], refs[2 : 2 + count], refs[2 + count :]
-    if start_sweep:
-        pq_hbm, w_hbm, acc_ref, near_ref, far_ref, lon_ref, lat_ref, pq_ref, sems = refs
-        mine = lax.axis_index("lon") & half
-        far = pltpu.make_async_copy(w_hbm.at[pl.ds(half - mine, half)], far_ref, sems.at[0])
-        near = pltpu.make_async_copy(w_hbm.at[pl.ds(mine, half)], near_ref, sems.at[1])
-        parts = pltpu.make_async_copy(pq_hbm.at[pl.ds(1, 2)], pq_ref, sems.at[2])
-        for copy in (parts, far, near):
-            copy.start()
-    else:
-        near_ref, far_ref, acc_ref = refs
+    mine = lax.axis_index("lon") & half
+    far = pltpu.make_async_copy(w_hbm.at[pl.ds(half - mine, half)], far_ref, sems.at[0])
+    near = pltpu.make_async_copy(w_hbm.at[pl.ds(mine, half)], near_ref, sems.at[1])
+    parts = pltpu.make_async_copy(pq_hbm.at[pl.ds(1, 2)], pq_ref, sems.at[2])
+    for copy in (parts, far, near):
+        copy.start()
+    parts.wait()
+    to_tiles(pq_ref.at[0], lon_ref)
+    to_tiles(pq_ref.at[1], lat_ref)
+    far.wait()
+    near.wait()
+
+
+def early_kernel(n_lon, *refs):
+    targets_ref, moved_ref, near_ref, far_ref = refs[:4]
+    x_refs, acc_ref = refs[4:-1], refs[-1]
     acc_ref[...] = moved_ref[0 : acc_ref.shape[0], :]
-    if start_sweep:
-        parts.wait()
-        to_tiles(pq_ref.at[0], lon_ref)
-        to_tiles(pq_ref.at[1], lat_ref)
-        far.wait()
-        near.wait()
-    add_sources(n_lon, partners, targets_ref, x_refs, near_ref, far_ref, acc_ref)
+    add_sources(n_lon, groups(n_lon)[0], targets_ref, x_refs, near_ref, far_ref, acc_ref)
 
 
 def late_kernel(n_lat, n_lon, start_sweep, *refs):
     partners = groups(n_lon)[1]
     count = len(partners)
-    targets_ref, coef_ref, moved_ref, near_ref, far_ref = refs[:5]
+    targets_ref, coef_ref, _, near_ref, far_ref = refs[:5]
     x_refs, refs = refs[5 : 5 + count], refs[5 + count :]
     if start_sweep:
         monitor_ref, balance_ref, pay_ref, acc_ref = refs
@@ -191,7 +189,6 @@
         det_ref, monitor_ref, balance_ref, pay_ref, acc_ref = refs
     rows, cols = monitor_ref.shape
     blocks = cols // TILE
-    acc_ref[...] = jnp.zeros_like(acc_ref)
     add_sources(n_lon, partners, targets_ref, x_refs, near_ref, far_ref, acc_ref)
 
     field_id = lax.broadcasted_iota(jnp.int32, (FIELDS, TILE), 0)
@@ -204,7 +201,7 @@
             for i in range(8):
                 start = ((b * 8 + i) * blocks + c) * FIELDS
                 place = slice(start, start + FIELDS)
-                blended = moved_ref[place, :] + acc_ref[place, :]
+                blended = acc_ref[place, :]
                 parts.append(coef * (blended * blended))
             monitor_ref[b * 8 : b * 8 + 8, c * TILE : (c + 1) * TILE] = jnp.sqrt(
                 1.0 + sum_fields(parts)
@@ -441,39 +438,43 @@
         early, late = ([got[r] for r in group] for group in groups(n_lon))
         start_sweep = det is None
         if start_sweep:
-            args = [in_hbm(pq), in_hbm(weights)]
-            out_shape = (acc_shape, half_shape, half_shape, acc_shape, acc_shape)
-            scratch = [
-                pltpu.VMEM((2,) + pq.shape[1:], pq.dtype),
-                pltpu.SemaphoreType.DMA((3,)),
-            ]
-        else:
-            args, out_shape, scratch = list(kept[:2]), (acc_shape,), []
-        base, *fetched = pl.pallas_call(
-            functools.partial(early_kernel, n_lon, start_sweep),
-            out_shape=out_shape,
-            in_specs=[smem]
-            + [vmem] * (1 + len(early))
-            + [hbm if start_sweep else vmem] * len(args),
-            out_specs=(vmem,) * len(out_shape),
-            scratch_shapes=scratch,
+            kept = pl.pallas_call(
+                functools.partial(fetch_kernel, n_lon),
+                out_shape=(half_shape, half_shape, acc_shape, acc_shape),
+                in_specs=[hbm] * 2,
+                out_specs=(vmem,) * 4,
+                scratch_shapes=[
+                    pltpu.VMEM((2,) + pq.shape[1:], pq.dtype),
+                    pltpu.SemaphoreType.DMA((3,)),
+                ],
+                compiler_params=params,
+                cost_estimate=pl.CostEstimate(
+                    flops=1 << 20, bytes_accessed=10 << 20, transcendentals=0
+                ),
+                name="fetch",
+            )(in_hbm(pq), in_hbm(weights))
+        base = pl.pallas_call(
+            functools.partial(early_kernel, n_lon),
+            out_shape=acc_shape,
+            in_specs=[smem] + [vmem] * (3 + len(early)),
+            out_specs=vmem,
             compiler_params=params,
             cost_estimate=early_cost,
             name="early",
-        )(targets, moved, *early, *args)
-        kept = fetched if start_sweep else kept
+        )(targets, moved, *kept[:2], *early)
         pay_width = TILE + (cols if start_sweep else 2 * cols)
-        out_shape = (grid, grid, jax.ShapeDtypeStruct((n_dev, 1, pay_width), f32))
+        out_shape = (grid, grid, jax.ShapeDtypeStruct((n_dev, 1, pay_width), f32), acc_shape)
         args = [targets, coef, base, *kept[:2], *late] + ([] if start_sweep else [det])
         outs = pl.pallas_call(
             functools.partial(late_kernel, n_lat, n_lon, start_sweep),
             out_shape=out_shape,
             in_specs=[smem, smem] + [vmem] * (len(args) - 2),
-            out_specs=(vmem,) * 3,
-            scratch_shapes=[pltpu.VMEM((tile_rows, TILE), f32)],
+            out_specs=(vmem,) * 4,
+            input_output_aliases={2: 3},
             compiler_params=params,
             name="late",
         )(*args)
+        outs = outs[:3]
         return (*outs, kept)
 
     def share(pay):

time: 91.9 us -> 91.8 us (level)
    pallas_call x3 -> x4, Pallas kernels: 7.93 us -> 7.95 us  [the longest x3 4.15 us: interp(): pl.pallas_call(functools.partial(early_kernel, n_lon), out_shape=acc_shap...]
  transfers between devices with their start and end apart: 21 -> 21, of which waited for: 10 -> 9; matrix products, arithmetic and copies ran while one was open for 0% -> 0% of each run, Pallas kernels for 9% -> 9%
where the time goes in v1:
time: 91.8 us; the launch traced here: 91.6 us
  blocking collectives  31.5 us (34%)
  starting transfers between devices  25.1 us (27%)
  Pallas kernels  19.3 us (21%)
  waiting for transfers between devices  14.8 us (16%)
    all_to_all x3, blocking collectives, share(): return lax.all_to_all(pay, ('lat', 'lon'), 0, 0, tiled=True)  31.5 us
    ppermute x21, starting transfers between devices, interp(): got[r] = lax.ppermute(send[r], 'lon', [(i, i ^ r) for i in range(n_lon)])  25.1 us
    ppermute x21, waiting for transfers between devices, interp(): got[r] = lax.ppermute(send[r], 'lon', [(i, i ^ r) for i in range(n_lon)])  14.8 us
    pallas_call x3, Pallas kernels, interp(): pl.pallas_call(functools.partial(late_kernel, n_lat, n_lon, start_sweep),...  5.52 us
    pallas_call x3, Pallas kernels, interp(): pl.pallas_call(functools.partial(early_kernel, n_lon), out_shape=acc_shap...  4.15 us
    pallas_call x1, Pallas kernels, interp(): pl.pallas_call(functools.partial(fetch_kernel, n_lon), out_shape=(half_sh...  3.79 us
    pallas_call x2, Pallas kernels, per_device(): pl.pallas_call(functools.partial(update_kernel, n_lat, n_lon, len(gots)),...  3.25 us
  transfers between devices with their start and end apart: 21, of which 9 were waited for; matrix products, arithmetic and copies ran while one was open for 0% of the time, Pallas kernels for 9%

profile of v1, /device:TPU:0, one launch (start us, length us, event | category | flops | bytes accessed | tf_op | source)
XLA Modules:
  0.0 91.6 jit_solution(6156699046208007474)
XLA Ops:
  0.6 1.7 %first.1 = (f32[2056,128]{1,0:T(8,128)S(1)}, s32[8,32]{1,0:T(8,128)S(1)}, s32[8,32]{1,0:T(8,128)S(1)}, f32[8]{0:T(128)S(1)}, bf16[256,128]{1,0:T(8,128)(2,1)S(1)...) custom-call(s32[8,32]{1,0:T(8,128)} %bitcast.5, ...), custom_call_target="tpu_custom_call" | custom-call | tf_op jit(solution)/shard_map/first/pallas_call | solution.py:412
  2.9 4.7 %collective-permute-start.1 = (bf16[256,128]{1,0:T(8,128)(2,1)S(1)}, bf16[256,128]{1,0:T(8,128)(2,1)S(1)}, u32[]{:S(2)}, u32[]{:S(2)}) collective-permute-start(bf16[256,128]{1,0:T(8,128)(2,1)S(1)} %get-tuple-element.57), channel_id=1, source_target_pairs={{0,7},{1,6},{2,5},{3,4},{4,3},{5,2},{6,1},{7,0},{8,15},{9,14},{10,... | collective-permute-start | bytes 196616 | tf_op jit(solution)/shard_map/ppermute | solution.py:437
  7.6 1.4 %collective-permute-start.4 = (bf16[256,128]{1,0:T(8,128)(2,1)S(1)}, bf16[256,128]{1,0:T(8,128)(2,1)S(1)}, u32[]{:S(2)}, u32[]{:S(2)}) collective-permute-start(bf16[256,128]{1,0:T(8,128)(2,1)S(1)} %get-tuple-element.60), channel_id=1, source_target_pairs={{0,3},{1,2},{2,1},{3,0},{4,7},{5,6},{6,5},{7,4},{8,11},{9,10},{10,... | collective-permute-start | bytes 196616 | tf_op jit(solution)/shard_map/ppermute | solution.py:437
  9.0 2.9 %collective-permute-start.5 = (bf16[256,128]{1,0:T(8,128)(2,1)S(1)}, bf16[256,128]{1,0:T(8,128)(2,1)S(1)}, u32[]{:S(2)}, u32[]{:S(2)}) collective-permute-start(bf16[256,128]{1,0:T(8,128)(2,1)S(1)} %get-tuple-element.61), channel_id=1, source_target_pairs={{0,4},{1,5},{2,6},{3,7},{4,0},{5,1},{6,2},{7,3},{8,12},{9,13},{10,... | collective-permute-start | bytes 196616 | tf_op jit(solution)/shard_map/ppermute | solution.py:437
  12.0 3.8 %fetch.1 = (bf16[4,32,128,128]{3,2,1,0:T(8,128)(2,1)S(1)}, bf16[4,32,128,128]{3,2,1,0:T(8,128)(2,1)S(1)}, f32[2048,128]{1,0:T(8,128)S(1)}, f32[2048,128]{1,0:T(8,128)S(1)}) custom-call(bf16[3,8,64,512]{3,2,1,0:T(8,128)(2,1)} %refs_0_.1, bf16[8,32,128,128]{3,2,1,0:T(8,128)(2,1)} %bitcast.4), custom_call_target="tpu_custom_call" | custom-call | flops 1048576 | bytes 10485760 | tf_op jit(solution)/shard_map/fetch/pallas_call | solution.py:441
  15.8 1.4 %early.3.refs_2_ = f32[2048,128]{1,0:T(8,128)S(1)} custom-call(s32[8,32]{1,0:T(8,128)S(1)} %get-tuple-element.49.refs_0_, f32[2056,128]{1,0:T(8,128)S(1)} %get-tuple-element.52.refs_1_.refs_4_.refs_6_, bf16[4,32,128,128]{3,2,1,0:T(8,128)(2,1)S(1)} %get-tuple-element.53.refs_2_.refs_3_, bf16[4,32,128,128]{3,2,1,0:T(8,128)(2,1)S(1)} %get-tuple-element.54.refs_3_.refs_4_, ...), custom_call_target="tpu_custom_call" | custom-call | flops 33554432 | bytes 4194304 | tf_op jit(solution)/shard_map/early/pallas_call | solution.py:456
  17.2 2.8 %collective-permute-done.6.refs_8_ = bf16[256,128]{1,0:T(8,128)(2,1)S(1)} collective-permute-done((bf16[256,128]{1,0:T(8,128)(2,1)S(1)}, bf16[256,128]{1,0:T(8,128)(2,1)S(1)}, u32[]{:S(2)}, u32[]{:S(2)}) %collective-permute-start.6) | collective-permute-done | bytes 65568 | tf_op jit(solution)/shard_map/ppermute | solution.py:437
  20.0 1.8 %late.3 = (f32[64,512]{1,0:T(8,128)S(1)}, f32[64,512]{1,0:T(8,128)S(1)}, f32[32,1,640]{2,1,0:T(1,128)S(1)}, f32[2048,128]{1,0:T(8,128)S(1)}) custom-call(s32[8,32]{1,0:T(8,128)S(1)} %get-tuple-element.49.refs_0_, f32[8]{0:T(128)S(1)} %get-tuple-element.50.refs_1_, f32[2048,128]{1,0:T(8,128)S(1)} %early.3.refs_2_, ...), custom_call_target="tpu_custom_call", output_to_operand_aliasing={{3}: (2, {})} | custom-call | tf_op jit(solution)/shard_map/late/pallas_call | solution.py:468
  21.9 12.2 %all_to_all.15.refs_1_ = f32[32,1,640]{2,1,0:T(1,128)S(1)} all-to-all(f32[32,1,640]{2,1,0:T(1,128)S(1)} %get-tuple-element.63), channel_id=1, replica_groups=mesh['lat'=4,'lon'=8] {'lat','lon'}, dimensions={0} | all-to-all | bytes 163840 | tf_op jit(solution)/shard_map/all_to_all | solution.py:481
  34.1 1.6 %update.2 = (f32[64,512]{1,0:T(8,128)S(1)}, f32[64,512]{1,0:T(8,128)S(1)}, f32[2056,128]{1,0:T(8,128)S(1)}, bf16[256,128]{1,0:T(8,128)(2,1)S(1)}, bf16[256,128]{...) custom-call(s32[8,32]{1,0:T(8,128)S(1)} %get-tuple-element.51.refs_0, ...), custom_call_target="tpu_custom_call" | custom-call | tf_op jit(solution)/shard_map/update/pallas_call | solution.py:493
  36.7 3.0 %collective-permute-start.9 = (bf16[256,128]{1,0:T(8,128)(2,1)S(1)}, bf16[256,128]{1,0:T(8,128)(2,1)S(1)}, u32[]{:S(2)}, u32[]{:S(2)}) collective-permute-start(bf16[256,128]{1,0:T(8,128)(2,1)S(1)} %get-tuple-element.72), channel_id=1, source_target_pairs={{0,6},{1,7},{2,4},{3,5},{4,2},{5,3},{6,0},{7,1},{8,14},{9,15},{10,... | collective-permute-start | bytes 196616 | tf_op jit(solution)/shard_map/ppermute | solution.py:437
  41.6 2.5 %collective-permute-start.13 = (bf16[256,128]{1,0:T(8,128)(2,1)S(1)}, bf16[256,128]{1,0:T(8,128)(2,1)S(1)}, u32[]{:S(2)}, u32[]{:S(2)}) collective-permute-start(bf16[256,128]{1,0:T(8,128)(2,1)S(1)} %get-tuple-element.76), channel_id=1, source_target_pairs={{0,5},{1,4},{2,7},{3,6},{4,1},{5,0},{6,3},{7,2},{8,13},{9,12},{10,... | collective-permute-start | bytes 196616 | tf_op jit(solution)/shard_map/ppermute | solution.py:437
  45.5 1.9 %collective-permute-done.11.refs_6_ = bf16[256,128]{1,0:T(8,128)(2,1)S(1)} collective-permute-done((bf16[256,128]{1,0:T(8,128)(2,1)S(1)}, bf16[256,128]{1,0:T(8,128)(2,1)S(1)}, u32[]{:S(2)}, u32[]{:S(2)}) %collective-permute-start.11) | collective-permute-done | bytes 65568 | tf_op jit(solution)/shard_map/ppermute | solution.py:437
  47.4 2.2 %collective-permute-done.12.refs_7_ = bf16[256,128]{1,0:T(8,128)(2,1)S(1)} collective-permute-done((bf16[256,128]{1,0:T(8,128)(2,1)S(1)}, bf16[256,128]{1,0:T(8,128)(2,1)S(1)}, u32[]{:S(2)}, u32[]{:S(2)}) %collective-permute-start.12) | collective-permute-done | bytes 65568 | tf_op jit(solution)/shard_map/ppermute | solution.py:437
  50.9 1.9 %late.4 = (f32[64,512]{1,0:T(8,128)S(1)}, f32[64,512]{1,0:T(8,128)S(1)}, f32[32,1,1152]{2,1,0:T(1,128)S(1)}, f32[2048,128]{1,0:T(8,128)S(1)}) custom-call(s32[8,32]{1,0:T(8,128)S(1)} %get-tuple-element.49.refs_0_, f32[8]{0:T(128)S(1)} %get-tuple-element.50.refs_1_, f32[2048,128]{1,0:T(8,128)S(1)} %early.4.refs_2_, ...), custom_call_target="tpu_custom_call", output_to_operand_aliasing={{3}: (2, {})} | custom-call | tf_op jit(solution)/shard_map/late/pallas_call | solution.py:468
  52.8 10.1 %all_to_all.16.refs_2_ = f32[32,1,1152]{2,1,0:T(1,128)S(1)} all-to-all(f32[32,1,1152]{2,1,0:T(1,128)S(1)} %get-tuple-element.78), channel_id=1, replica_groups=mesh['lat'=4,'lon'=8] {'lat','lon'}, dimensions={0} | all-to-all | bytes 294912 | tf_op jit(solution)/shard_map/all_to_all | solution.py:481
  62.8 1.6 %update.3 = (f32[64,512]{1,0:T(8,128)S(1)}, f32[64,512]{1,0:T(8,128)S(1)}, f32[2056,128]{1,0:T(8,128)S(1)}, bf16[256,128]{1,0:T(8,128)(2,1)S(1)}, bf16[256,128]{...) custom-call(s32[8,32]{1,0:T(8,128)S(1)} %get-tuple-element.51.refs_0, ...), custom_call_target="tpu_custom_call" | custom-call | tf_op jit(solution)/shard_map/update/pallas_call | solution.py:493
  65.6 2.9 %collective-permute-start.16 = (bf16[256,128]{1,0:T(8,128)(2,1)S(1)}, bf16[256,128]{1,0:T(8,128)(2,1)S(1)}, u32[]{:S(2)}, u32[]{:S(2)}) collective-permute-start(bf16[256,128]{1,0:T(8,128)(2,1)S(1)} %get-tuple-element.86), channel_id=1, source_target_pairs={{0,6},{1,7},{2,4},{3,5},{4,2},{5,3},{6,0},{7,1},{8,14},{9,15},{10,... | collective-permute-start | bytes 196616 | tf_op jit(solution)/shard_map/ppermute | solution.py:437
  68.5 1.4 %collective-permute-start.18 = (bf16[256,128]{1,0:T(8,128)(2,1)S(1)}, bf16[256,128]{1,0:T(8,128)(2,1)S(1)}, u32[]{:S(2)}, u32[]{:S(2)}) collective-permute-start(bf16[256,128]{1,0:T(8,128)(2,1)S(1)} %get-tuple-element.88), channel_id=1, source_target_pairs={{0,3},{1,2},{2,1},{3,0},{4,7},{5,6},{6,5},{7,4},{8,11},{9,10},{10,... | collective-permute-start | bytes 196616 | tf_op jit(solution)/shard_map/ppermute | solution.py:437
  70.9 2.0 %collective-permute-start.20 = (bf16[256,128]{1,0:T(8,128)(2,1)S(1)}, bf16[256,128]{1,0:T(8,128)(2,1)S(1)}, u32[]{:S(2)}, u32[]{:S(2)}) collective-permute-start(bf16[256,128]{1,0:T(8,128)(2,1)S(1)} %get-tuple-element.90), channel_id=1, source_target_pairs={{0,5},{1,4},{2,7},{3,6},{4,1},{5,0},{6,3},{7,2},{8,13},{9,12},{10,... | collective-permute-start | bytes 196616 | tf_op jit(solution)/shard_map/ppermute | solution.py:437
  74.3 2.4 %collective-permute-done.18.refs_6_ = bf16[256,128]{1,0:T(8,128)(2,1)S(1)} collective-permute-done((bf16[256,128]{1,0:T(8,128)(2,1)S(1)}, bf16[256,128]{1,0:T(8,128)(2,1)S(1)}, u32[]{:S(2)}, u32[]{:S(2)}) %collective-permute-start.18) | collective-permute-done | bytes 65568 | tf_op jit(solution)/shard_map/ppermute | solution.py:437
  76.7 1.9 %collective-permute-done.19.refs_7_ = bf16[256,128]{1,0:T(8,128)(2,1)S(1)} collective-permute-done((bf16[256,128]{1,0:T(8,128)(2,1)S(1)}, bf16[256,128]{1,0:T(8,128)(2,1)S(1)}, u32[]{:S(2)}, u32[]{:S(2)}) %collective-permute-start.19) | collective-permute-done | bytes 65568 | tf_op jit(solution)/shard_map/ppermute | solution.py:437
  79.5 1.8 %late.5 = (f32[64,512]{1,0:T(8,128)S(1)}, f32[64,512]{1,0:T(8,128)S(1)}, f32[32,1,1152]{2,1,0:T(1,128)S(1)}, f32[2048,128]{1,0:T(8,128)S(1)}) custom-call(s32[8,32]{1,0:T(8,128)S(1)} %get-tuple-element.49.refs_0_, f32[8]{0:T(128)S(1)} %get-tuple-element.50.refs_1_, f32[2048,128]{1,0:T(8,128)S(1)} %early.5.refs_2_, ...), custom_call_target="tpu_custom_call", output_to_operand_aliasing={{3}: (2, {})} | custom-call | tf_op jit(solution)/shard_map/late/pallas_call | solution.py:468
  81.4 9.2 %all_to_all.17.got_ref = f32[32,1,128]{2,1,0:T(1,128)S(1)} all-to-all(f32[32,1,128]{2,1,0:T(1,128)S(1)} %slice.3), channel_id=1, replica_groups=mesh['lat'=4,'lon'=8] {'lat','lon'}, dimensions={0} | all-to-all | bytes 32768 | tf_op jit(solution)/shard_map/all_to_all | solution.py:481
  (33 shorter events, 11.6 us)
Async XLA Ops:
  2.3 6.7 %collective-permute-start = (bf16[256,128]{1,0:T(8,128)(2,1)S(1)}, bf16[256,128]{1,0:T(8,128)(2,1)S(1)}, u32[]{:S(2)}, u32[]{:S(2)}) collective-permute-start(bf16[256,128]{1,0:T(8,128)(2,1)S(1)} %get-tuple-element.56), channel_id=1, source_target_pairs={{0,1},{1,0},{2,3},{3,2},{4,5},{5,4},{6,7},{7,6},{8,9},{9,8},{10,11... | collective-permute-start | bytes 196616 | tf_op jit(solution)/shard_map/ppermute | solution.py:437
  2.9 9.1 %collective-permute-start.1 = (bf16[256,128]{1,0:T(8,128)(2,1)S(1)}, bf16[256,128]{1,0:T(8,128)(2,1)S(1)}, u32[]{:S(2)}, u32[]{:S(2)}) collective-permute-start(bf16[256,128]{1,0:T(8,128)(2,1)S(1)} %get-tuple-element.57), channel_id=1, source_target_pairs={{0,7},{1,6},{2,5},{3,4},{4,3},{5,2},{6,1},{7,0},{8,15},{9,14},{10,... | collective-permute-start | bytes 196616 | tf_op jit(solution)/shard_map/ppermute | solution.py:437
  7.6 8.2 %collective-permute-start.2 = (bf16[256,128]{1,0:T(8,128)(2,1)S(1)}, bf16[256,128]{1,0:T(8,128)(2,1)S(1)}, u32[]{:S(2)}, u32[]{:S(2)}) collective-permute-start(bf16[256,128]{1,0:T(8,128)(2,1)S(1)} %get-tuple-element.58), channel_id=1, source_target_pairs={{0,6},{1,7},{2,4},{3,5},{4,2},{5,3},{6,0},{7,1},{8,14},{9,15},{10,... | collective-permute-start | bytes 196616 | tf_op jit(solution)/shard_map/ppermute | solution.py:437
  7.6 9.6 %collective-permute-start.3 = (bf16[256,128]{1,0:T(8,128)(2,1)S(1)}, bf16[256,128]{1,0:T(8,128)(2,1)S(1)}, u32[]{:S(2)}, u32[]{:S(2)}) collective-permute-start(bf16[256,128]{1,0:T(8,128)(2,1)S(1)} %get-tuple-element.59), channel_id=1, source_target_pairs={{0,2},{1,3},{2,0},{3,1},{4,6},{5,7},{6,4},{7,5},{8,10},{9,11},{10,... | collective-permute-start | bytes 196616 | tf_op jit(solution)/shard_map/ppermute | solution.py:437
  7.6 9.6 %collective-permute-start.4 = (bf16[256,128]{1,0:T(8,128)(2,1)S(1)}, bf16[256,128]{1,0:T(8,128)(2,1)S(1)}, u32[]{:S(2)}, u32[]{:S(2)}) collective-permute-start(bf16[256,128]{1,0:T(8,128)(2,1)S(1)} %get-tuple-element.60), channel_id=1, source_target_pairs={{0,3},{1,2},{2,1},{3,0},{4,7},{5,6},{6,5},{7,4},{8,11},{9,10},{10,... | collective-permute-start | bytes 196616 | tf_op jit(solution)/shard_map/ppermute | solution.py:437
  9.0 8.2 %collective-permute-start.5 = (bf16[256,128]{1,0:T(8,128)(2,1)S(1)}, bf16[256,128]{1,0:T(8,128)(2,1)S(1)}, u32[]{:S(2)}, u32[]{:S(2)}) collective-permute-start(bf16[256,128]{1,0:T(8,128)(2,1)S(1)} %get-tuple-element.61), channel_id=1, source_target_pairs={{0,4},{1,5},{2,6},{3,7},{4,0},{5,1},{6,2},{7,3},{8,12},{9,13},{10,... | collective-permute-start | bytes 196616 | tf_op jit(solution)/shard_map/ppermute | solution.py:437
  12.0 8.1 %collective-permute-start.6 = (bf16[256,128]{1,0:T(8,128)(2,1)S(1)}, bf16[256,128]{1,0:T(8,128)(2,1)S(1)}, u32[]{:S(2)}, u32[]{:S(2)}) collective-permute-start(bf16[256,128]{1,0:T(8,128)(2,1)S(1)} %get-tuple-element.62), channel_id=1, source_target_pairs={{0,5},{1,4},{2,7},{3,6},{4,1},{5,0},{6,3},{7,2},{8,13},{9,12},{10,... | collective-permute-start | bytes 196616 | tf_op jit(solution)/shard_map/ppermute | solution.py:437
  35.7 5.2 %collective-permute-start.7 = (bf16[256,128]{1,0:T(8,128)(2,1)S(1)}, bf16[256,128]{1,0:T(8,128)(2,1)S(1)}, u32[]{:S(2)}, u32[]{:S(2)}) collective-permute-start(bf16[256,128]{1,0:T(8,128)(2,1)S(1)} %get-tuple-element.70), channel_id=1, source_target_pairs={{0,1},{1,0},{2,3},{3,2},{4,5},{5,4},{6,7},{7,6},{8,9},{9,8},{10,11... | collective-permute-start | bytes 196616 | tf_op jit(solution)/shard_map/ppermute | solution.py:437
  35.9 5.7 %collective-permute-start.8 = (bf16[256,128]{1,0:T(8,128)(2,1)S(1)}, bf16[256,128]{1,0:T(8,128)(2,1)S(1)}, u32[]{:S(2)}, u32[]{:S(2)}) collective-permute-start(bf16[256,128]{1,0:T(8,128)(2,1)S(1)} %get-tuple-element.71), channel_id=1, source_target_pairs={{0,7},{1,6},{2,5},{3,4},{4,3},{5,2},{6,1},{7,0},{8,15},{9,14},{10,... | collective-permute-start | bytes 196616 | tf_op jit(solution)/shard_map/ppermute | solution.py:437
  36.7 7.4 %collective-permute-start.9 = (bf16[256,128]{1,0:T(8,128)(2,1)S(1)}, bf16[256,128]{1,0:T(8,128)(2,1)S(1)}, u32[]{:S(2)}, u32[]{:S(2)}) collective-permute-start(bf16[256,128]{1,0:T(8,128)(2,1)S(1)} %get-tuple-element.72), channel_id=1, source_target_pairs={{0,6},{1,7},{2,4},{3,5},{4,2},{5,3},{6,0},{7,1},{8,14},{9,15},{10,... | collective-permute-start | bytes 196616 | tf_op jit(solution)/shard_map/ppermute | solution.py:437
  39.7 5.8 %collective-permute-start.10 = (bf16[256,128]{1,0:T(8,128)(2,1)S(1)}, bf16[256,128]{1,0:T(8,128)(2,1)S(1)}, u32[]{:S(2)}, u32[]{:S(2)}) collective-permute-start(bf16[256,128]{1,0:T(8,128)(2,1)S(1)} %get-tuple-element.73), channel_id=1, source_target_pairs={{0,2},{1,3},{2,0},{3,1},{4,6},{5,7},{6,4},{7,5},{8,10},{9,11},{10,... | collective-permute-start | bytes 196616 | tf_op jit(solution)/shard_map/ppermute | solution.py:437
  39.7 7.7 %collective-permute-start.11 = (bf16[256,128]{1,0:T(8,128)(2,1)S(1)}, bf16[256,128]{1,0:T(8,128)(2,1)S(1)}, u32[]{:S(2)}, u32[]{:S(2)}) collective-permute-start(bf16[256,128]{1,0:T(8,128)(2,1)S(1)} %get-tuple-element.74), channel_id=1, source_target_pairs={{0,3},{1,2},{2,1},{3,0},{4,7},{5,6},{6,5},{7,4},{8,11},{9,10},{10,... | collective-permute-start | bytes 196616 | tf_op jit(solution)/shard_map/ppermute | solution.py:437
  40.9 8.7 %collective-permute-start.12 = (bf16[256,128]{1,0:T(8,128)(2,1)S(1)}, bf16[256,128]{1,0:T(8,128)(2,1)S(1)}, u32[]{:S(2)}, u32[]{:S(2)}) collective-permute-start(bf16[256,128]{1,0:T(8,128)(2,1)S(1)} %get-tuple-element.75), channel_id=1, source_target_pairs={{0,4},{1,5},{2,6},{3,7},{4,0},{5,1},{6,2},{7,3},{8,12},{9,13},{10,... | collective-permute-start | bytes 196616 | tf_op jit(solution)/shard_map/ppermute | solution.py:437
  41.6 9.3 %collective-permute-start.13 = (bf16[256,128]{1,0:T(8,128)(2,1)S(1)}, bf16[256,128]{1,0:T(8,128)(2,1)S(1)}, u32[]{:S(2)}, u32[]{:S(2)}) collective-permute-start(bf16[256,128]{1,0:T(8,128)(2,1)S(1)} %get-tuple-element.76), channel_id=1, source_target_pairs={{0,5},{1,4},{2,7},{3,6},{4,1},{5,0},{6,3},{7,2},{8,13},{9,12},{10,... | collective-permute-start | bytes 196616 | tf_op jit(solution)/shard_map/ppermute | solution.py:437
  64.5 5.4 %collective-permute-start.14 = (bf16[256,128]{1,0:T(8,128)(2,1)S(1)}, bf16[256,128]{1,0:T(8,128)(2,1)S(1)}, u32[]{:S(2)}, u32[]{:S(2)}) collective-permute-start(bf16[256,128]{1,0:T(8,128)(2,1)S(1)} %get-tuple-element.84), channel_id=1, source_target_pairs={{0,1},{1,0},{2,3},{3,2},{4,5},{5,4},{6,7},{7,6},{8,9},{9,8},{10,11... | collective-permute-start | bytes 196616 | tf_op jit(solution)/shard_map/ppermute | solution.py:437
  64.9 6.0 %collective-permute-start.15 = (bf16[256,128]{1,0:T(8,128)(2,1)S(1)}, bf16[256,128]{1,0:T(8,128)(2,1)S(1)}, u32[]{:S(2)}, u32[]{:S(2)}) collective-permute-start(bf16[256,128]{1,0:T(8,128)(2,1)S(1)} %get-tuple-element.85), channel_id=1, source_target_pairs={{0,7},{1,6},{2,5},{3,4},{4,3},{5,2},{6,1},{7,0},{8,15},{9,14},{10,... | collective-permute-start | bytes 196616 | tf_op jit(solution)/shard_map/ppermute | solution.py:437
  65.6 7.3 %collective-permute-start.16 = (bf16[256,128]{1,0:T(8,128)(2,1)S(1)}, bf16[256,128]{1,0:T(8,128)(2,1)S(1)}, u32[]{:S(2)}, u32[]{:S(2)}) collective-permute-start(bf16[256,128]{1,0:T(8,128)(2,1)S(1)} %get-tuple-element.86), channel_id=1, source_target_pairs={{0,6},{1,7},{2,4},{3,5},{4,2},{5,3},{6,0},{7,1},{8,14},{9,15},{10,... | collective-permute-start | bytes 196616 | tf_op jit(solution)/shard_map/ppermute | solution.py:437
  68.5 5.8 %collective-permute-start.17 = (bf16[256,128]{1,0:T(8,128)(2,1)S(1)}, bf16[256,128]{1,0:T(8,128)(2,1)S(1)}, u32[]{:S(2)}, u32[]{:S(2)}) collective-permute-start(bf16[256,128]{1,0:T(8,128)(2,1)S(1)} %get-tuple-element.87), channel_id=1, source_target_pairs={{0,2},{1,3},{2,0},{3,1},{4,6},{5,7},{6,4},{7,5},{8,10},{9,11},{10,... | collective-permute-start | bytes 196616 | tf_op jit(solution)/shard_map/ppermute | solution.py:437
  68.5 8.2 %collective-permute-start.18 = (bf16[256,128]{1,0:T(8,128)(2,1)S(1)}, bf16[256,128]{1,0:T(8,128)(2,1)S(1)}, u32[]{:S(2)}, u32[]{:S(2)}) collective-permute-start(bf16[256,128]{1,0:T(8,128)(2,1)S(1)} %get-tuple-element.88), channel_id=1, source_target_pairs={{0,3},{1,2},{2,1},{3,0},{4,7},{5,6},{6,5},{7,4},{8,11},{9,10},{10,... | collective-permute-start | bytes 196616 | tf_op jit(solution)/shard_map/ppermute | solution.py:437
  69.9 8.7 %collective-permute-start.19 = (bf16[256,128]{1,0:T(8,128)(2,1)S(1)}, bf16[256,128]{1,0:T(8,128)(2,1)S(1)}, u32[]{:S(2)}, u32[]{:S(2)}) collective-permute-start(bf16[256,128]{1,0:T(8,128)(2,1)S(1)} %get-tuple-element.89), channel_id=1, source_target_pairs={{0,4},{1,5},{2,6},{3,7},{4,0},{5,1},{6,2},{7,3},{8,12},{9,13},{10,... | collective-permute-start | bytes 196616 | tf_op jit(solution)/shard_map/ppermute | solution.py:437
  70.9 8.6 %collective-permute-start.20 = (bf16[256,128]{1,0:T(8,128)(2,1)S(1)}, bf16[256,128]{1,0:T(8,128)(2,1)S(1)}, u32[]{:S(2)}, u32[]{:S(2)}) collective-permute-start(bf16[256,128]{1,0:T(8,128)(2,1)S(1)} %get-tuple-element.90), channel_id=1, source_target_pairs={{0,5},{1,4},{2,7},{3,6},{4,1},{5,0},{6,3},{7,2},{8,13},{9,12},{10,... | collective-permute-start | bytes 196616 | tf_op jit(solution)/shard_map/ppermute | solution.py:437

commit v2 on v1

--- a/solution.py
+++ b/solution.py
@@ -259,11 +259,12 @@
     total = got_ref[0, :, stat_at : stat_at + TILE]
     for j in range(1, n_dev):
         total = total + got_ref[j, :, stat_at : stat_at + TILE]
-    target = lane_value(total, 0) / n_dev
+    centre = total / n_dev
     apart = jnp.zeros((1, TILE), jnp.float32)
     for j in range(n_dev):
-        away = got_ref[j, :, stat_at : stat_at + TILE] - target
+        away = got_ref[j, :, stat_at : stat_at + TILE] - centre
         apart = apart + away * away
+    target = lane_value(centre, 0)
     variance = (lane_value(total, 1) / count + lane_value(apart, 0)) / n_dev
     return target, jnp.sqrt(variance + 1e-06)
 

time: 91.8 us -> 91.6 us (level)
  no operation moved by 1% of the time
where the time goes in v2:
time: 91.6 us; the launch traced here: 91.4 us
  blocking collectives  31.5 us (34%)
  starting transfers between devices  25.1 us (27%)
  Pallas kernels  19.1 us (21%)
  waiting for transfers between devices  14.8 us (16%)
    all_to_all x3, blocking collectives, share(): return lax.all_to_all(pay, ('lat', 'lon'), 0, 0, tiled=True)  31.5 us
    ppermute x21, starting transfers between devices, interp(): got[r] = lax.ppermute(send[r], 'lon', [(i, i ^ r) for i in range(n_lon)])  25.1 us
    ppermute x21, waiting for transfers between devices, interp(): got[r] = lax.ppermute(send[r], 'lon', [(i, i ^ r) for i in range(n_lon)])  14.8 us
    pallas_call x3, Pallas kernels, interp(): pl.pallas_call(functools.partial(late_kernel, n_lat, n_lon, start_sweep),...  5.52 us
    pallas_call x3, Pallas kernels, interp(): pl.pallas_call(functools.partial(early_kernel, n_lon), out_shape=acc_shap...  4.15 us
    pallas_call x1, Pallas kernels, interp(): pl.pallas_call(functools.partial(fetch_kernel, n_lon), out_shape=(half_sh...  3.79 us
    pallas_call x2, Pallas kernels, per_device(): pl.pallas_call(functools.partial(update_kernel, n_lat, n_lon, len(gots)),...  3.12 us
  transfers between devices with their start and end apart: 21, of which 9 were waited for; matrix products, arithmetic and copies ran while one was open for 0% of the time, Pallas kernels for 9%

profile of v2, /device:TPU:0, one launch (start us, length us, event | category | flops | bytes accessed | tf_op | source)
XLA Modules:
  0.0 91.4 jit_solution(6969313870150705541)
XLA Ops:
  0.6 1.7 %first.1 = (f32[2056,128]{1,0:T(8,128)S(1)}, s32[8,32]{1,0:T(8,128)S(1)}, s32[8,32]{1,0:T(8,128)S(1)}, f32[8]{0:T(128)S(1)}, bf16[256,128]{1,0:T(8,128)(2,1)S(1)...) custom-call(s32[8,32]{1,0:T(8,128)} %bitcast.5, ...), custom_call_target="tpu_custom_call" | custom-call | tf_op jit(solution)/shard_map/first/pallas_call | solution.py:413
  2.9 4.7 %collective-permute-start.1 = (bf16[256,128]{1,0:T(8,128)(2,1)S(1)}, bf16[256,128]{1,0:T(8,128)(2,1)S(1)}, u32[]{:S(2)}, u32[]{:S(2)}) collective-permute-start(bf16[256,128]{1,0:T(8,128)(2,1)S(1)} %get-tuple-element.57), channel_id=1, source_target_pairs={{0,7},{1,6},{2,5},{3,4},{4,3},{5,2},{6,1},{7,0},{8,15},{9,14},{10,... | collective-permute-start | bytes 196616 | tf_op jit(solution)/shard_map/ppermute | solution.py:438
  7.6 1.4 %collective-permute-start.4 = (bf16[256,128]{1,0:T(8,128)(2,1)S(1)}, bf16[256,128]{1,0:T(8,128)(2,1)S(1)}, u32[]{:S(2)}, u32[]{:S(2)}) collective-permute-start(bf16[256,128]{1,0:T(8,128)(2,1)S(1)} %get-tuple-element.60), channel_id=1, source_target_pairs={{0,3},{1,2},{2,1},{3,0},{4,7},{5,6},{6,5},{7,4},{8,11},{9,10},{10,... | collective-permute-start | bytes 196616 | tf_op jit(solution)/shard_map/ppermute | solution.py:438
  9.0 2.9 %collective-permute-start.5 = (bf16[256,128]{1,0:T(8,128)(2,1)S(1)}, bf16[256,128]{1,0:T(8,128)(2,1)S(1)}, u32[]{:S(2)}, u32[]{:S(2)}) collective-permute-start(bf16[256,128]{1,0:T(8,128)(2,1)S(1)} %get-tuple-element.61), channel_id=1, source_target_pairs={{0,4},{1,5},{2,6},{3,7},{4,0},{5,1},{6,2},{7,3},{8,12},{9,13},{10,... | collective-permute-start | bytes 196616 | tf_op jit(solution)/shard_map/ppermute | solution.py:438
  12.0 3.8 %fetch.1 = (bf16[4,32,128,128]{3,2,1,0:T(8,128)(2,1)S(1)}, bf16[4,32,128,128]{3,2,1,0:T(8,128)(2,1)S(1)}, f32[2048,128]{1,0:T(8,128)S(1)}, f32[2048,128]{1,0:T(8,128)S(1)}) custom-call(bf16[3,8,64,512]{3,2,1,0:T(8,128)(2,1)} %refs_0_.1, bf16[8,32,128,128]{3,2,1,0:T(8,128)(2,1)} %bitcast.4), custom_call_target="tpu_custom_call" | custom-call | flops 1048576 | bytes 10485760 | tf_op jit(solution)/shard_map/fetch/pallas_call | solution.py:442
  15.8 1.4 %early.3.refs_2_ = f32[2048,128]{1,0:T(8,128)S(1)} custom-call(s32[8,32]{1,0:T(8,128)S(1)} %get-tuple-element.49.refs_0_, f32[2056,128]{1,0:T(8,128)S(1)} %get-tuple-element.52.refs_1_.refs_4_.refs_6_, bf16[4,32,128,128]{3,2,1,0:T(8,128)(2,1)S(1)} %get-tuple-element.53.refs_2_.refs_3_, bf16[4,32,128,128]{3,2,1,0:T(8,128)(2,1)S(1)} %get-tuple-element.54.refs_3_.refs_4_, ...), custom_call_target="tpu_custom_call" | custom-call | flops 33554432 | bytes 4194304 | tf_op jit(solution)/shard_map/early/pallas_call | solution.py:457
  17.2 2.8 %collective-permute-done.6.refs_8_ = bf16[256,128]{1,0:T(8,128)(2,1)S(1)} collective-permute-done((bf16[256,128]{1,0:T(8,128)(2,1)S(1)}, bf16[256,128]{1,0:T(8,128)(2,1)S(1)}, u32[]{:S(2)}, u32[]{:S(2)}) %collective-permute-start.6) | collective-permute-done | bytes 65568 | tf_op jit(solution)/shard_map/ppermute | solution.py:438
  20.0 1.8 %late.3 = (f32[64,512]{1,0:T(8,128)S(1)}, f32[64,512]{1,0:T(8,128)S(1)}, f32[32,1,640]{2,1,0:T(1,128)S(1)}, f32[2048,128]{1,0:T(8,128)S(1)}) custom-call(s32[8,32]{1,0:T(8,128)S(1)} %get-tuple-element.49.refs_0_, f32[8]{0:T(128)S(1)} %get-tuple-element.50.refs_1_, f32[2048,128]{1,0:T(8,128)S(1)} %early.3.refs_2_, ...), custom_call_target="tpu_custom_call", output_to_operand_aliasing={{3}: (2, {})} | custom-call | tf_op jit(solution)/shard_map/late/pallas_call | solution.py:469
  21.9 12.2 %all_to_all.15.refs_1_ = f32[32,1,640]{2,1,0:T(1,128)S(1)} all-to-all(f32[32,1,640]{2,1,0:T(1,128)S(1)} %get-tuple-element.63), channel_id=1, replica_groups=mesh['lat'=4,'lon'=8] {'lat','lon'}, dimensions={0} | all-to-all | bytes 163840 | tf_op jit(solution)/shard_map/all_to_all | solution.py:482
  34.1 1.5 %update.2 = (f32[64,512]{1,0:T(8,128)S(1)}, f32[64,512]{1,0:T(8,128)S(1)}, f32[2056,128]{1,0:T(8,128)S(1)}, bf16[256,128]{1,0:T(8,128)(2,1)S(1)}, bf16[256,128]{...) custom-call(s32[8,32]{1,0:T(8,128)S(1)} %get-tuple-element.51.refs_0, ...), custom_call_target="tpu_custom_call" | custom-call | tf_op jit(solution)/shard_map/update/pallas_call | solution.py:494
  36.6 3.0 %collective-permute-start.9 = (bf16[256,128]{1,0:T(8,128)(2,1)S(1)}, bf16[256,128]{1,0:T(8,128)(2,1)S(1)}, u32[]{:S(2)}, u32[]{:S(2)}) collective-permute-start(bf16[256,128]{1,0:T(8,128)(2,1)S(1)} %get-tuple-element.72), channel_id=1, source_target_pairs={{0,6},{1,7},{2,4},{3,5},{4,2},{5,3},{6,0},{7,1},{8,14},{9,15},{10,... | collective-permute-start | bytes 196616 | tf_op jit(solution)/shard_map/ppermute | solution.py:438
  41.5 2.5 %collective-permute-start.13 = (bf16[256,128]{1,0:T(8,128)(2,1)S(1)}, bf16[256,128]{1,0:T(8,128)(2,1)S(1)}, u32[]{:S(2)}, u32[]{:S(2)}) collective-permute-start(bf16[256,128]{1,0:T(8,128)(2,1)S(1)} %get-tuple-element.76), channel_id=1, source_target_pairs={{0,5},{1,4},{2,7},{3,6},{4,1},{5,0},{6,3},{7,2},{8,13},{9,12},{10,... | collective-permute-start | bytes 196616 | tf_op jit(solution)/shard_map/ppermute | solution.py:438
  45.4 1.9 %collective-permute-done.11.refs_6_ = bf16[256,128]{1,0:T(8,128)(2,1)S(1)} collective-permute-done((bf16[256,128]{1,0:T(8,128)(2,1)S(1)}, bf16[256,128]{1,0:T(8,128)(2,1)S(1)}, u32[]{:S(2)}, u32[]{:S(2)}) %collective-permute-start.11) | collective-permute-done | bytes 65568 | tf_op jit(solution)/shard_map/ppermute | solution.py:438
  47.3 2.2 %collective-permute-done.12.refs_7_ = bf16[256,128]{1,0:T(8,128)(2,1)S(1)} collective-permute-done((bf16[256,128]{1,0:T(8,128)(2,1)S(1)}, bf16[256,128]{1,0:T(8,128)(2,1)S(1)}, u32[]{:S(2)}, u32[]{:S(2)}) %collective-permute-start.12) | collective-permute-done | bytes 65568 | tf_op jit(solution)/shard_map/ppermute | solution.py:438
  50.8 1.9 %late.4 = (f32[64,512]{1,0:T(8,128)S(1)}, f32[64,512]{1,0:T(8,128)S(1)}, f32[32,1,1152]{2,1,0:T(1,128)S(1)}, f32[2048,128]{1,0:T(8,128)S(1)}) custom-call(s32[8,32]{1,0:T(8,128)S(1)} %get-tuple-element.49.refs_0_, f32[8]{0:T(128)S(1)} %get-tuple-element.50.refs_1_, f32[2048,128]{1,0:T(8,128)S(1)} %early.4.refs_2_, ...), custom_call_target="tpu_custom_call", output_to_operand_aliasing={{3}: (2, {})} | custom-call | tf_op jit(solution)/shard_map/late/pallas_call | solution.py:469
  52.7 10.1 %all_to_all.16.refs_2_ = f32[32,1,1152]{2,1,0:T(1,128)S(1)} all-to-all(f32[32,1,1152]{2,1,0:T(1,128)S(1)} %get-tuple-element.78), channel_id=1, replica_groups=mesh['lat'=4,'lon'=8] {'lat','lon'}, dimensions={0} | all-to-all | bytes 294912 | tf_op jit(solution)/shard_map/all_to_all | solution.py:482
  62.8 1.6 %update.3 = (f32[64,512]{1,0:T(8,128)S(1)}, f32[64,512]{1,0:T(8,128)S(1)}, f32[2056,128]{1,0:T(8,128)S(1)}, bf16[256,128]{1,0:T(8,128)(2,1)S(1)}, bf16[256,128]{...) custom-call(s32[8,32]{1,0:T(8,128)S(1)} %get-tuple-element.51.refs_0, ...), custom_call_target="tpu_custom_call" | custom-call | tf_op jit(solution)/shard_map/update/pallas_call | solution.py:494
  65.5 2.9 %collective-permute-start.16 = (bf16[256,128]{1,0:T(8,128)(2,1)S(1)}, bf16[256,128]{1,0:T(8,128)(2,1)S(1)}, u32[]{:S(2)}, u32[]{:S(2)}) collective-permute-start(bf16[256,128]{1,0:T(8,128)(2,1)S(1)} %get-tuple-element.86), channel_id=1, source_target_pairs={{0,6},{1,7},{2,4},{3,5},{4,2},{5,3},{6,0},{7,1},{8,14},{9,15},{10,... | collective-permute-start | bytes 196616 | tf_op jit(solution)/shard_map/ppermute | solution.py:438
  68.4 1.4 %collective-permute-start.18 = (bf16[256,128]{1,0:T(8,128)(2,1)S(1)}, bf16[256,128]{1,0:T(8,128)(2,1)S(1)}, u32[]{:S(2)}, u32[]{:S(2)}) collective-permute-start(bf16[256,128]{1,0:T(8,128)(2,1)S(1)} %get-tuple-element.88), channel_id=1, source_target_pairs={{0,3},{1,2},{2,1},{3,0},{4,7},{5,6},{6,5},{7,4},{8,11},{9,10},{10,... | collective-permute-start | bytes 196616 | tf_op jit(solution)/shard_map/ppermute | solution.py:438
  70.8 2.0 %collective-permute-start.20 = (bf16[256,128]{1,0:T(8,128)(2,1)S(1)}, bf16[256,128]{1,0:T(8,128)(2,1)S(1)}, u32[]{:S(2)}, u32[]{:S(2)}) collective-permute-start(bf16[256,128]{1,0:T(8,128)(2,1)S(1)} %get-tuple-element.90), channel_id=1, source_target_pairs={{0,5},{1,4},{2,7},{3,6},{4,1},{5,0},{6,3},{7,2},{8,13},{9,12},{10,... | collective-permute-start | bytes 196616 | tf_op jit(solution)/shard_map/ppermute | solution.py:438
  74.2 2.4 %collective-permute-done.18.refs_6_ = bf16[256,128]{1,0:T(8,128)(2,1)S(1)} collective-permute-done((bf16[256,128]{1,0:T(8,128)(2,1)S(1)}, bf16[256,128]{1,0:T(8,128)(2,1)S(1)}, u32[]{:S(2)}, u32[]{:S(2)}) %collective-permute-start.18) | collective-permute-done | bytes 65568 | tf_op jit(solution)/shard_map/ppermute | solution.py:438
  76.5 1.9 %collective-permute-done.19.refs_7_ = bf16[256,128]{1,0:T(8,128)(2,1)S(1)} collective-permute-done((bf16[256,128]{1,0:T(8,128)(2,1)S(1)}, bf16[256,128]{1,0:T(8,128)(2,1)S(1)}, u32[]{:S(2)}, u32[]{:S(2)}) %collective-permute-start.19) | collective-permute-done | bytes 65568 | tf_op jit(solution)/shard_map/ppermute | solution.py:438
  79.4 1.8 %late.5 = (f32[64,512]{1,0:T(8,128)S(1)}, f32[64,512]{1,0:T(8,128)S(1)}, f32[32,1,1152]{2,1,0:T(1,128)S(1)}, f32[2048,128]{1,0:T(8,128)S(1)}) custom-call(s32[8,32]{1,0:T(8,128)S(1)} %get-tuple-element.49.refs_0_, f32[8]{0:T(128)S(1)} %get-tuple-element.50.refs_1_, f32[2048,128]{1,0:T(8,128)S(1)} %early.5.refs_2_, ...), custom_call_target="tpu_custom_call", output_to_operand_aliasing={{3}: (2, {})} | custom-call | tf_op jit(solution)/shard_map/late/pallas_call | solution.py:469
  81.2 9.2 %all_to_all.17.got_ref = f32[32,1,128]{2,1,0:T(1,128)S(1)} all-to-all(f32[32,1,128]{2,1,0:T(1,128)S(1)} %slice.3), channel_id=1, replica_groups=mesh['lat'=4,'lon'=8] {'lat','lon'}, dimensions={0} | all-to-all | bytes 32768 | tf_op jit(solution)/shard_map/all_to_all | solution.py:482
  (33 shorter events, 11.6 us)
Async XLA Ops:
  2.3 6.7 %collective-permute-start = (bf16[256,128]{1,0:T(8,128)(2,1)S(1)}, bf16[256,128]{1,0:T(8,128)(2,1)S(1)}, u32[]{:S(2)}, u32[]{:S(2)}) collective-permute-start(bf16[256,128]{1,0:T(8,128)(2,1)S(1)} %get-tuple-element.56), channel_id=1, source_target_pairs={{0,1},{1,0},{2,3},{3,2},{4,5},{5,4},{6,7},{7,6},{8,9},{9,8},{10,11... | collective-permute-start | bytes 196616 | tf_op jit(solution)/shard_map/ppermute | solution.py:438
  2.9 9.1 %collective-permute-start.1 = (bf16[256,128]{1,0:T(8,128)(2,1)S(1)}, bf16[256,128]{1,0:T(8,128)(2,1)S(1)}, u32[]{:S(2)}, u32[]{:S(2)}) collective-permute-start(bf16[256,128]{1,0:T(8,128)(2,1)S(1)} %get-tuple-element.57), channel_id=1, source_target_pairs={{0,7},{1,6},{2,5},{3,4},{4,3},{5,2},{6,1},{7,0},{8,15},{9,14},{10,... | collective-permute-start | bytes 196616 | tf_op jit(solution)/shard_map/ppermute | solution.py:438
  7.6 8.2 %collective-permute-start.2 = (bf16[256,128]{1,0:T(8,128)(2,1)S(1)}, bf16[256,128]{1,0:T(8,128)(2,1)S(1)}, u32[]{:S(2)}, u32[]{:S(2)}) collective-permute-start(bf16[256,128]{1,0:T(8,128)(2,1)S(1)} %get-tuple-element.58), channel_id=1, source_target_pairs={{0,6},{1,7},{2,4},{3,5},{4,2},{5,3},{6,0},{7,1},{8,14},{9,15},{10,... | collective-permute-start | bytes 196616 | tf_op jit(solution)/shard_map/ppermute | solution.py:438
  7.6 9.6 %collective-permute-start.3 = (bf16[256,128]{1,0:T(8,128)(2,1)S(1)}, bf16[256,128]{1,0:T(8,128)(2,1)S(1)}, u32[]{:S(2)}, u32[]{:S(2)}) collective-permute-start(bf16[256,128]{1,0:T(8,128)(2,1)S(1)} %get-tuple-element.59), channel_id=1, source_target_pairs={{0,2},{1,3},{2,0},{3,1},{4,6},{5,7},{6,4},{7,5},{8,10},{9,11},{10,... | collective-permute-start | bytes 196616 | tf_op jit(solution)/shard_map/ppermute | solution.py:438
  7.6 9.6 %collective-permute-start.4 = (bf16[256,128]{1,0:T(8,128)(2,1)S(1)}, bf16[256,128]{1,0:T(8,128)(2,1)S(1)}, u32[]{:S(2)}, u32[]{:S(2)}) collective-permute-start(bf16[256,128]{1,0:T(8,128)(2,1)S(1)} %get-tuple-element.60), channel_id=1, source_target_pairs={{0,3},{1,2},{2,1},{3,0},{4,7},{5,6},{6,5},{7,4},{8,11},{9,10},{10,... | collective-permute-start | bytes 196616 | tf_op jit(solution)/shard_map/ppermute | solution.py:438
  9.0 8.2 %collective-permute-start.5 = (bf16[256,128]{1,0:T(8,128)(2,1)S(1)}, bf16[256,128]{1,0:T(8,128)(2,1)S(1)}, u32[]{:S(2)}, u32[]{:S(2)}) collective-permute-start(bf16[256,128]{1,0:T(8,128)(2,1)S(1)} %get-tuple-element.61), channel_id=1, source_target_pairs={{0,4},{1,5},{2,6},{3,7},{4,0},{5,1},{6,2},{7,3},{8,12},{9,13},{10,... | collective-permute-start | bytes 196616 | tf_op jit(solution)/shard_map/ppermute | solution.py:438
  12.0 8.1 %collective-permute-start.6 = (bf16[256,128]{1,0:T(8,128)(2,1)S(1)}, bf16[256,128]{1,0:T(8,128)(2,1)S(1)}, u32[]{:S(2)}, u32[]{:S(2)}) collective-permute-start(bf16[256,128]{1,0:T(8,128)(2,1)S(1)} %get-tuple-element.62), channel_id=1, source_target_pairs={{0,5},{1,4},{2,7},{3,6},{4,1},{5,0},{6,3},{7,2},{8,13},{9,12},{10,... | collective-permute-start | bytes 196616 | tf_op jit(solution)/shard_map/ppermute | solution.py:438
  35.6 5.2 %collective-permute-start.7 = (bf16[256,128]{1,0:T(8,128)(2,1)S(1)}, bf16[256,128]{1,0:T(8,128)(2,1)S(1)}, u32[]{:S(2)}, u32[]{:S(2)}) collective-permute-start(bf16[256,128]{1,0:T(8,128)(2,1)S(1)} %get-tuple-element.70), channel_id=1, source_target_pairs={{0,1},{1,0},{2,3},{3,2},{4,5},{5,4},{6,7},{7,6},{8,9},{9,8},{10,11... | collective-permute-start | bytes 196616 | tf_op jit(solution)/shard_map/ppermute | solution.py:438
  35.8 5.7 %collective-permute-start.8 = (bf16[256,128]{1,0:T(8,128)(2,1)S(1)}, bf16[256,128]{1,0:T(8,128)(2,1)S(1)}, u32[]{:S(2)}, u32[]{:S(2)}) collective-permute-start(bf16[256,128]{1,0:T(8,128)(2,1)S(1)} %get-tuple-element.71), channel_id=1, source_target_pairs={{0,7},{1,6},{2,5},{3,4},{4,3},{5,2},{6,1},{7,0},{8,15},{9,14},{10,... | collective-permute-start | bytes 196616 | tf_op jit(solution)/shard_map/ppermute | solution.py:438
  36.6 7.4 %collective-permute-start.9 = (bf16[256,128]{1,0:T(8,128)(2,1)S(1)}, bf16[256,128]{1,0:T(8,128)(2,1)S(1)}, u32[]{:S(2)}, u32[]{:S(2)}) collective-permute-start(bf16[256,128]{1,0:T(8,128)(2,1)S(1)} %get-tuple-element.72), channel_id=1, source_target_pairs={{0,6},{1,7},{2,4},{3,5},{4,2},{5,3},{6,0},{7,1},{8,14},{9,15},{10,... | collective-permute-start | bytes 196616 | tf_op jit(solution)/shard_map/ppermute | solution.py:438
  39.6 5.8 %collective-permute-start.10 = (bf16[256,128]{1,0:T(8,128)(2,1)S(1)}, bf16[256,128]{1,0:T(8,128)(2,1)S(1)}, u32[]{:S(2)}, u32[]{:S(2)}) collective-permute-start(bf16[256,128]{1,0:T(8,128)(2,1)S(1)} %get-tuple-element.73), channel_id=1, source_target_pairs={{0,2},{1,3},{2,0},{3,1},{4,6},{5,7},{6,4},{7,5},{8,10},{9,11},{10,... | collective-permute-start | bytes 196616 | tf_op jit(solution)/shard_map/ppermute | solution.py:438
  39.6 7.7 %collective-permute-start.11 = (bf16[256,128]{1,0:T(8,128)(2,1)S(1)}, bf16[256,128]{1,0:T(8,128)(2,1)S(1)}, u32[]{:S(2)}, u32[]{:S(2)}) collective-permute-start(bf16[256,128]{1,0:T(8,128)(2,1)S(1)} %get-tuple-element.74), channel_id=1, source_target_pairs={{0,3},{1,2},{2,1},{3,0},{4,7},{5,6},{6,5},{7,4},{8,11},{9,10},{10,... | collective-permute-start | bytes 196616 | tf_op jit(solution)/shard_map/ppermute | solution.py:438
  40.8 8.7 %collective-permute-start.12 = (bf16[256,128]{1,0:T(8,128)(2,1)S(1)}, bf16[256,128]{1,0:T(8,128)(2,1)S(1)}, u32[]{:S(2)}, u32[]{:S(2)}) collective-permute-start(bf16[256,128]{1,0:T(8,128)(2,1)S(1)} %get-tuple-element.75), channel_id=1, source_target_pairs={{0,4},{1,5},{2,6},{3,7},{4,0},{5,1},{6,2},{7,3},{8,12},{9,13},{10,... | collective-permute-start | bytes 196616 | tf_op jit(solution)/shard_map/ppermute | solution.py:438
  41.5 9.3 %collective-permute-start.13 = (bf16[256,128]{1,0:T(8,128)(2,1)S(1)}, bf16[256,128]{1,0:T(8,128)(2,1)S(1)}, u32[]{:S(2)}, u32[]{:S(2)}) collective-permute-start(bf16[256,128]{1,0:T(8,128)(2,1)S(1)} %get-tuple-element.76), channel_id=1, source_target_pairs={{0,5},{1,4},{2,7},{3,6},{4,1},{5,0},{6,3},{7,2},{8,13},{9,12},{10,... | collective-permute-start | bytes 196616 | tf_op jit(solution)/shard_map/ppermute | solution.py:438
  64.4 5.4 %collective-permute-start.14 = (bf16[256,128]{1,0:T(8,128)(2,1)S(1)}, bf16[256,128]{1,0:T(8,128)(2,1)S(1)}, u32[]{:S(2)}, u32[]{:S(2)}) collective-permute-start(bf16[256,128]{1,0:T(8,128)(2,1)S(1)} %get-tuple-element.84), channel_id=1, source_target_pairs={{0,1},{1,0},{2,3},{3,2},{4,5},{5,4},{6,7},{7,6},{8,9},{9,8},{10,11... | collective-permute-start | bytes 196616 | tf_op jit(solution)/shard_map/ppermute | solution.py:438
  64.8 6.0 %collective-permute-start.15 = (bf16[256,128]{1,0:T(8,128)(2,1)S(1)}, bf16[256,128]{1,0:T(8,128)(2,1)S(1)}, u32[]{:S(2)}, u32[]{:S(2)}) collective-permute-start(bf16[256,128]{1,0:T(8,128)(2,1)S(1)} %get-tuple-element.85), channel_id=1, source_target_pairs={{0,7},{1,6},{2,5},{3,4},{4,3},{5,2},{6,1},{7,0},{8,15},{9,14},{10,... | collective-permute-start | bytes 196616 | tf_op jit(solution)/shard_map/ppermute | solution.py:438
  65.5 7.3 %collective-permute-start.16 = (bf16[256,128]{1,0:T(8,128)(2,1)S(1)}, bf16[256,128]{1,0:T(8,128)(2,1)S(1)}, u32[]{:S(2)}, u32[]{:S(2)}) collective-permute-start(bf16[256,128]{1,0:T(8,128)(2,1)S(1)} %get-tuple-element.86), channel_id=1, source_target_pairs={{0,6},{1,7},{2,4},{3,5},{4,2},{5,3},{6,0},{7,1},{8,14},{9,15},{10,... | collective-permute-start | bytes 196616 | tf_op jit(solution)/shard_map/ppermute | solution.py:438
  68.4 5.8 %collective-permute-start.17 = (bf16[256,128]{1,0:T(8,128)(2,1)S(1)}, bf16[256,128]{1,0:T(8,128)(2,1)S(1)}, u32[]{:S(2)}, u32[]{:S(2)}) collective-permute-start(bf16[256,128]{1,0:T(8,128)(2,1)S(1)} %get-tuple-element.87), channel_id=1, source_target_pairs={{0,2},{1,3},{2,0},{3,1},{4,6},{5,7},{6,4},{7,5},{8,10},{9,11},{10,... | collective-permute-start | bytes 196616 | tf_op jit(solution)/shard_map/ppermute | solution.py:438
  68.4 8.2 %collective-permute-start.18 = (bf16[256,128]{1,0:T(8,128)(2,1)S(1)}, bf16[256,128]{1,0:T(8,128)(2,1)S(1)}, u32[]{:S(2)}, u32[]{:S(2)}) collective-permute-start(bf16[256,128]{1,0:T(8,128)(2,1)S(1)} %get-tuple-element.88), channel_id=1, source_target_pairs={{0,3},{1,2},{2,1},{3,0},{4,7},{5,6},{6,5},{7,4},{8,11},{9,10},{10,... | collective-permute-start | bytes 196616 | tf_op jit(solution)/shard_map/ppermute | solution.py:438
  69.8 8.7 %collective-permute-start.19 = (bf16[256,128]{1,0:T(8,128)(2,1)S(1)}, bf16[256,128]{1,0:T(8,128)(2,1)S(1)}, u32[]{:S(2)}, u32[]{:S(2)}) collective-permute-start(bf16[256,128]{1,0:T(8,128)(2,1)S(1)} %get-tuple-element.89), channel_id=1, source_target_pairs={{0,4},{1,5},{2,6},{3,7},{4,0},{5,1},{6,2},{7,3},{8,12},{9,13},{10,... | collective-permute-start | bytes 196616 | tf_op jit(solution)/shard_map/ppermute | solution.py:438
  70.8 8.6 %collective-permute-start.20 = (bf16[256,128]{1,0:T(8,128)(2,1)S(1)}, bf16[256,128]{1,0:T(8,128)(2,1)S(1)}, u32[]{:S(2)}, u32[]{:S(2)}) collective-permute-start(bf16[256,128]{1,0:T(8,128)(2,1)S(1)} %get-tuple-element.90), channel_id=1, source_target_pairs={{0,5},{1,4},{2,7},{3,6},{4,1},{5,0},{6,3},{7,2},{8,13},{9,12},{10,... | collective-permute-start | bytes 196616 | tf_op jit(solution)/shard_map/ppermute | solution.py:438
